TPU v7x, 256 devices: a whole 4x4x8 slice. The times are simulated.
256 devices in a mesh: row: 16 (over z, core), col: 16 (over y, x).
Axes of the slice: x: 4, y: 4, z: 8, core: 2. Of those that a mesh axis runs over, the one named last changes fastest.
Arguments:
- sigma_anc: float32 [48, 48, 128, 128], P('row', 'col'), as said below
- factor: float32 [16, 256, 128, 128], P('row', 'col'), may hold values from -1.25 to 1.25
- diag_inv: float32 [256, 128, 128], P('col'), as said below
- struct: int32 [256, 16], P('col'), may hold values from 0 to 47, all different within a row
Outputs:
- z_off: float32 [256, 48, 128, 128], P('col', 'row')
- z_diag: float32 [256, 128, 128], P(('col', 'row'))
Inputs may be any that keep to these rules, and one draw needn't show every extreme that they name: Each row of struct names 16 different ancestor blocks, and every ancestor block is named by some row. sigma_anc is symmetric: block [b, a] is the transpose of block [a, b]. Each diag_inv[k] is lower triangular with a positive diagonal.
All inputs are finite; a program needn't handle non-finite values.
Results may differ from a plain program's by a relative error of at most 0.0003.
Values sent between devices are 32-bit elements; how exact they have to be, the bound alone decides.
A program may use at most 128 MiB of HBM per device.

v0:
```python
import jax
import jax.numpy as jnp
from jax import lax
from jax.sharding import PartitionSpec as P

highest = lax.Precision.HIGHEST


def select_blocks(sigma_rows, slot_ids):
    return jnp.take(sigma_rows, slot_ids, axis=1)


def body(sigma_anc, factor, diag_inv, struct):
    row_count = sigma_anc.shape[0]
    node_count = diag_inv.shape[0]
    width = diag_inv.shape[1]
    row_index = lax.axis_index("row")
    own_rows = row_index * row_count + jnp.arange(row_count, dtype=jnp.int32)
    sigma_rows = lax.all_gather(sigma_anc, "col", axis=1, tiled=True)
    u_local = jnp.einsum("skij,kjl->skil", factor, diag_inv, precision=highest)
    empty = jnp.zeros((node_count, row_count, width, width), jnp.float32)

    def one_slot(running, element):
        u_slot, id_slot = element
        y_sum, u_rows = running
        picked = select_blocks(sigma_rows, id_slot)
        y_sum = y_sum + jnp.einsum("akij,kjl->kail", picked, u_slot, precision=highest)
        match = (id_slot[:, None] == own_rows[None, :]).astype(jnp.float32)
        u_rows = u_rows + match[:, :, None, None] * u_slot[:, None, :, :]
        return ((y_sum, u_rows), None)

    result, unused_out = lax.scan(
        one_slot,
        (empty, empty),
        (lax.all_gather(u_local, "row", axis=0, tiled=True), jnp.transpose(struct)),
    )
    y_rows, u_rows = result
    member = jnp.any(struct[:, :, None] == own_rows[None, None, :], axis=1)
    z_off = jnp.where(member[:, :, None, None], -y_rows, 0.0)
    partial_sum = jnp.einsum("kaij,kail->kjl", u_rows, y_rows, precision=highest)
    share_count = node_count // lax.axis_size("row")
    start_node = row_index * share_count
    inverse_share = lax.dynamic_slice_in_dim(diag_inv, start_node, share_count, 0)
    inverse_part = jnp.einsum("kij,kil->kjl", inverse_share, inverse_share, precision=highest)
    summed = lax.psum(partial_sum, "row")
    mine = lax.dynamic_slice_in_dim(summed, start_node, share_count, 0)
    return (z_off, inverse_part + mine)


def solution(mesh):
    in_specs = (
        P("row", "col", None, None),
        P("row", "col", None, None),
        P("col", None, None),
        P("col", None),
    )
    out_specs = (P("col", "row", None, None), P(("col", "row"), None, None))
    return jax.shard_map(body, mesh=mesh, in_specs=in_specs, out_specs=out_specs, check_vma=False)
```

profile of v0, /device:TPU:1, one launch (start us, length us, event | category | flops | bytes accessed | tf_op | source)
XLA Modules:
  0.0 607.2 jit_solution(9201970120801829042)
XLA Ops:
  13.0 82.0 %all-gather.3.cloned.1.call-done = f32[3,48,128,128]{3,2,1,0:T(8,128)} async-done(((f32[3,3,128,128]{3,2,1,0:T(8,128)}), f32[3,48,128,128]{3,2,1,0:T(8,128)}) %all-gather.3.cloned.1.call-update) | async-done | bytes 9437200 | tf_op jit(solution)/shard_map/all_gather | solution.py:19
  95.0 97.4 %all-gather.5.cloned.1.call-done = f32[16,16,128,128]{3,2,1,0:T(8,128)} async-done(((f32[1,16,128,128]{3,2,1,0:T(8,128)}), f32[16,16,128,128]{3,2,1,0:T(8,128)}) %all-gather.5.cloned.1.call-update) | async-done | bytes 16777232 | tf_op jit(solution)/shard_map/all_gather | solution.py:35
  192.4 287.7 %while.13 = (s32[]{:T(128)}, f32[16,3,128,128]{3,2,1,0:T(8,128)}, f32[16,3,128,128]{3,2,1,0:T(8,128)}, s32[16,16]{1,0:T(8,128)S(1)}, f32[3,48,128,128]{3,2,1,0:T...) while((s32[]{:T(128)}, f32[16,3,128,128]{3,2,1,0:T(8,128)}, ...), condition=%wide.region_2.3_spmd.clone, body=%wide.region_1.2_spmd.clone.sunk | while | flops 1212679424 | bytes 26220016 | solution.py:32
  192.5 6.1 gather_fusion
  198.5 6.2 %select_add_fusion.4 = f32[16,3,128,128]{3,2,1,0:T(8,128)} fusion(f32[16,3,128,128]{3,2,1,0:T(8,128)} %get-tuple-element.149, f32[16,3,128,128]{3,2,1,0:T(8,128)} %gather_fusion, pred[16]{0:T(512)(128)(4,1)S(1)} %get-tuple-element.137, pred[]{:T(512)S(6)} %compare.3, f32[16,16,128,128]{3,2,1,0:T(8,128)} %get-tuple-element.162, s32[]{:T(128)} %get-tuple-element.148), kind=kOutput, calls=%fused_computation.5.clone.1 | convolution fusion | flops 1210318848 | bytes 10486289 | tf_op jit(solution)/shard_map/while/body/eval_jaxpr/akij,kjl->kail/dot_general | solution.py:27
  208.2 6.1 gather_fusion
  214.3 6.7 %select_add_fusion.4 = f32[16,3,128,128]{3,2,1,0:T(8,128)} fusion(f32[16,3,128,128]{3,2,1,0:T(8,128)} %get-tuple-element.149, f32[16,3,128,128]{3,2,1,0:T(8,128)} %gather_fusion, pred[16]{0:T(512)(128)(4,1)S(1)} %get-tuple-element.137, pred[]{:T(512)S(6)} %compare.3, f32[16,16,128,128]{3,2,1,0:T(8,128)} %get-tuple-element.162, s32[]{:T(128)} %get-tuple-element.148), kind=kOutput, calls=%fused_computation.5.clone.1 | convolution fusion | flops 1210318848 | bytes 10486289 | tf_op jit(solution)/shard_map/while/body/eval_jaxpr/akij,kjl->kail/dot_general | solution.py:27
  222.4 4.0 select_add_fusion.5
  226.4 6.1 gather_fusion
  232.4 6.7 %select_add_fusion.4 = f32[16,3,128,128]{3,2,1,0:T(8,128)} fusion(f32[16,3,128,128]{3,2,1,0:T(8,128)} %get-tuple-element.149, f32[16,3,128,128]{3,2,1,0:T(8,128)} %gather_fusion, pred[16]{0:T(512)(128)(4,1)S(1)} %get-tuple-element.137, pred[]{:T(512)S(6)} %compare.3, f32[16,16,128,128]{3,2,1,0:T(8,128)} %get-tuple-element.162, s32[]{:T(128)} %get-tuple-element.148), kind=kOutput, calls=%fused_computation.5.clone.1 | convolution fusion | flops 1210318848 | bytes 10486289 | tf_op jit(solution)/shard_map/while/body/eval_jaxpr/akij,kjl->kail/dot_general | solution.py:27
  240.5 4.0 select_add_fusion.5
  244.5 6.1 gather_fusion
  250.6 6.7 %select_add_fusion.4 = f32[16,3,128,128]{3,2,1,0:T(8,128)} fusion(f32[16,3,128,128]{3,2,1,0:T(8,128)} %get-tuple-element.149, f32[16,3,128,128]{3,2,1,0:T(8,128)} %gather_fusion, pred[16]{0:T(512)(128)(4,1)S(1)} %get-tuple-element.137, pred[]{:T(512)S(6)} %compare.3, f32[16,16,128,128]{3,2,1,0:T(8,128)} %get-tuple-element.162, s32[]{:T(128)} %get-tuple-element.148), kind=kOutput, calls=%fused_computation.5.clone.1 | convolution fusion | flops 1210318848 | bytes 10486289 | tf_op jit(solution)/shard_map/while/body/eval_jaxpr/akij,kjl->kail/dot_general | solution.py:27
  258.6 4.0 select_add_fusion.5
  262.6 6.1 gather_fusion
  268.7 6.7 %select_add_fusion.4 = f32[16,3,128,128]{3,2,1,0:T(8,128)} fusion(f32[16,3,128,128]{3,2,1,0:T(8,128)} %get-tuple-element.149, f32[16,3,128,128]{3,2,1,0:T(8,128)} %gather_fusion, pred[16]{0:T(512)(128)(4,1)S(1)} %get-tuple-element.137, pred[]{:T(512)S(6)} %compare.3, f32[16,16,128,128]{3,2,1,0:T(8,128)} %get-tuple-element.162, s32[]{:T(128)} %get-tuple-element.148), kind=kOutput, calls=%fused_computation.5.clone.1 | convolution fusion | flops 1210318848 | bytes 10486289 | tf_op jit(solution)/shard_map/while/body/eval_jaxpr/akij,kjl->kail/dot_general | solution.py:27
  276.8 4.0 select_add_fusion.5
  280.7 6.1 gather_fusion
  286.8 6.7 %select_add_fusion.4 = f32[16,3,128,128]{3,2,1,0:T(8,128)} fusion(f32[16,3,128,128]{3,2,1,0:T(8,128)} %get-tuple-element.149, f32[16,3,128,128]{3,2,1,0:T(8,128)} %gather_fusion, pred[16]{0:T(512)(128)(4,1)S(1)} %get-tuple-element.137, pred[]{:T(512)S(6)} %compare.3, f32[16,16,128,128]{3,2,1,0:T(8,128)} %get-tuple-element.162, s32[]{:T(128)} %get-tuple-element.148), kind=kOutput, calls=%fused_computation.5.clone.1 | convolution fusion | flops 1210318848 | bytes 10486289 | tf_op jit(solution)/shard_map/while/body/eval_jaxpr/akij,kjl->kail/dot_general | solution.py:27
  294.9 4.0 select_add_fusion.5
  298.9 6.1 gather_fusion
  305.0 6.7 %select_add_fusion.4 = f32[16,3,128,128]{3,2,1,0:T(8,128)} fusion(f32[16,3,128,128]{3,2,1,0:T(8,128)} %get-tuple-element.149, f32[16,3,128,128]{3,2,1,0:T(8,128)} %gather_fusion, pred[16]{0:T(512)(128)(4,1)S(1)} %get-tuple-element.137, pred[]{:T(512)S(6)} %compare.3, f32[16,16,128,128]{3,2,1,0:T(8,128)} %get-tuple-element.162, s32[]{:T(128)} %get-tuple-element.148), kind=kOutput, calls=%fused_computation.5.clone.1 | convolution fusion | flops 1210318848 | bytes 10486289 | tf_op jit(solution)/shard_map/while/body/eval_jaxpr/akij,kjl->kail/dot_general | solution.py:27
  313.0 4.0 select_add_fusion.5
  317.0 6.1 gather_fusion
  323.1 6.7 %select_add_fusion.4 = f32[16,3,128,128]{3,2,1,0:T(8,128)} fusion(f32[16,3,128,128]{3,2,1,0:T(8,128)} %get-tuple-element.149, f32[16,3,128,128]{3,2,1,0:T(8,128)} %gather_fusion, pred[16]{0:T(512)(128)(4,1)S(1)} %get-tuple-element.137, pred[]{:T(512)S(6)} %compare.3, f32[16,16,128,128]{3,2,1,0:T(8,128)} %get-tuple-element.162, s32[]{:T(128)} %get-tuple-element.148), kind=kOutput, calls=%fused_computation.5.clone.1 | convolution fusion | flops 1210318848 | bytes 10486289 | tf_op jit(solution)/shard_map/while/body/eval_jaxpr/akij,kjl->kail/dot_general | solution.py:27
  331.2 4.0 select_add_fusion.5
  335.1 6.1 gather_fusion
  341.2 6.7 %select_add_fusion.4 = f32[16,3,128,128]{3,2,1,0:T(8,128)} fusion(f32[16,3,128,128]{3,2,1,0:T(8,128)} %get-tuple-element.149, f32[16,3,128,128]{3,2,1,0:T(8,128)} %gather_fusion, pred[16]{0:T(512)(128)(4,1)S(1)} %get-tuple-element.137, pred[]{:T(512)S(6)} %compare.3, f32[16,16,128,128]{3,2,1,0:T(8,128)} %get-tuple-element.162, s32[]{:T(128)} %get-tuple-element.148), kind=kOutput, calls=%fused_computation.5.clone.1 | convolution fusion | flops 1210318848 | bytes 10486289 | tf_op jit(solution)/shard_map/while/body/eval_jaxpr/akij,kjl->kail/dot_general | solution.py:27
  349.3 4.0 select_add_fusion.5
  353.3 6.1 gather_fusion
  359.4 6.7 %select_add_fusion.4 = f32[16,3,128,128]{3,2,1,0:T(8,128)} fusion(f32[16,3,128,128]{3,2,1,0:T(8,128)} %get-tuple-element.149, f32[16,3,128,128]{3,2,1,0:T(8,128)} %gather_fusion, pred[16]{0:T(512)(128)(4,1)S(1)} %get-tuple-element.137, pred[]{:T(512)S(6)} %compare.3, f32[16,16,128,128]{3,2,1,0:T(8,128)} %get-tuple-element.162, s32[]{:T(128)} %get-tuple-element.148), kind=kOutput, calls=%fused_computation.5.clone.1 | convolution fusion | flops 1210318848 | bytes 10486289 | tf_op jit(solution)/shard_map/while/body/eval_jaxpr/akij,kjl->kail/dot_general | solution.py:27
  367.4 4.0 select_add_fusion.5
  371.4 6.1 gather_fusion
  377.5 6.7 %select_add_fusion.4 = f32[16,3,128,128]{3,2,1,0:T(8,128)} fusion(f32[16,3,128,128]{3,2,1,0:T(8,128)} %get-tuple-element.149, f32[16,3,128,128]{3,2,1,0:T(8,128)} %gather_fusion, pred[16]{0:T(512)(128)(4,1)S(1)} %get-tuple-element.137, pred[]{:T(512)S(6)} %compare.3, f32[16,16,128,128]{3,2,1,0:T(8,128)} %get-tuple-element.162, s32[]{:T(128)} %get-tuple-element.148), kind=kOutput, calls=%fused_computation.5.clone.1 | convolution fusion | flops 1210318848 | bytes 10486289 | tf_op jit(solution)/shard_map/while/body/eval_jaxpr/akij,kjl->kail/dot_general | solution.py:27
  385.6 4.0 select_add_fusion.5
  389.5 6.1 gather_fusion
  395.6 6.7 %select_add_fusion.4 = f32[16,3,128,128]{3,2,1,0:T(8,128)} fusion(f32[16,3,128,128]{3,2,1,0:T(8,128)} %get-tuple-element.149, f32[16,3,128,128]{3,2,1,0:T(8,128)} %gather_fusion, pred[16]{0:T(512)(128)(4,1)S(1)} %get-tuple-element.137, pred[]{:T(512)S(6)} %compare.3, f32[16,16,128,128]{3,2,1,0:T(8,128)} %get-tuple-element.162, s32[]{:T(128)} %get-tuple-element.148), kind=kOutput, calls=%fused_computation.5.clone.1 | convolution fusion | flops 1210318848 | bytes 10486289 | tf_op jit(solution)/shard_map/while/body/eval_jaxpr/akij,kjl->kail/dot_general | solution.py:27
  403.7 4.0 select_add_fusion.5
  407.7 6.1 gather_fusion
  413.8 6.7 %select_add_fusion.4 = f32[16,3,128,128]{3,2,1,0:T(8,128)} fusion(f32[16,3,128,128]{3,2,1,0:T(8,128)} %get-tuple-element.149, f32[16,3,128,128]{3,2,1,0:T(8,128)} %gather_fusion, pred[16]{0:T(512)(128)(4,1)S(1)} %get-tuple-element.137, pred[]{:T(512)S(6)} %compare.3, f32[16,16,128,128]{3,2,1,0:T(8,128)} %get-tuple-element.162, s32[]{:T(128)} %get-tuple-element.148), kind=kOutput, calls=%fused_computation.5.clone.1 | convolution fusion | flops 1210318848 | bytes 10486289 | tf_op jit(solution)/shard_map/while/body/eval_jaxpr/akij,kjl->kail/dot_general | solution.py:27
  425.8 6.1 gather_fusion
  431.9 6.7 %select_add_fusion.4 = f32[16,3,128,128]{3,2,1,0:T(8,128)} fusion(f32[16,3,128,128]{3,2,1,0:T(8,128)} %get-tuple-element.149, f32[16,3,128,128]{3,2,1,0:T(8,128)} %gather_fusion, pred[16]{0:T(512)(128)(4,1)S(1)} %get-tuple-element.137, pred[]{:T(512)S(6)} %compare.3, f32[16,16,128,128]{3,2,1,0:T(8,128)} %get-tuple-element.162, s32[]{:T(128)} %get-tuple-element.148), kind=kOutput, calls=%fused_computation.5.clone.1 | convolution fusion | flops 1210318848 | bytes 10486289 | tf_op jit(solution)/shard_map/while/body/eval_jaxpr/akij,kjl->kail/dot_general | solution.py:27
  443.9 6.1 gather_fusion
  450.0 6.7 %select_add_fusion.4 = f32[16,3,128,128]{3,2,1,0:T(8,128)} fusion(f32[16,3,128,128]{3,2,1,0:T(8,128)} %get-tuple-element.149, f32[16,3,128,128]{3,2,1,0:T(8,128)} %gather_fusion, pred[16]{0:T(512)(128)(4,1)S(1)} %get-tuple-element.137, pred[]{:T(512)S(6)} %compare.3, f32[16,16,128,128]{3,2,1,0:T(8,128)} %get-tuple-element.162, s32[]{:T(128)} %get-tuple-element.148), kind=kOutput, calls=%fused_computation.5.clone.1 | convolution fusion | flops 1210318848 | bytes 10486289 | tf_op jit(solution)/shard_map/while/body/eval_jaxpr/akij,kjl->kail/dot_general | solution.py:27
  462.1 6.1 gather_fusion
  468.2 6.7 %select_add_fusion.4 = f32[16,3,128,128]{3,2,1,0:T(8,128)} fusion(f32[16,3,128,128]{3,2,1,0:T(8,128)} %get-tuple-element.149, f32[16,3,128,128]{3,2,1,0:T(8,128)} %gather_fusion, pred[16]{0:T(512)(128)(4,1)S(1)} %get-tuple-element.137, pred[]{:T(512)S(6)} %compare.3, f32[16,16,128,128]{3,2,1,0:T(8,128)} %get-tuple-element.162, s32[]{:T(128)} %get-tuple-element.148), kind=kOutput, calls=%fused_computation.5.clone.1 | convolution fusion | flops 1210318848 | bytes 10486289 | tf_op jit(solution)/shard_map/while/body/eval_jaxpr/akij,kjl->kail/dot_general | solution.py:27
  480.2 9.0 %convolution_bitcast_fusion = f32[16,128,128]{2,1,0:T(8,128)} fusion(f32[16,3,128,128]{3,2,1,0:T(8,128)} %get-tuple-element.41, f32[16,3,128,128]{3,2,1,0:T(8,128)} %get-tuple-element.40), kind=kOutput, calls=%fused_computation.24 | convolution fusion | flops 1207959552 | bytes 7340032 | tf_op jit(solution)/shard_map/kaij,kail->kjl/dot_general | solution.py:40
  493.4 105.4 %all-reduce.2.cloned.1.call-done = f32[16,128,128]{2,1,0:T(8,128)} async-done(((f32[16,128,128]{2,1,0:T(8,128)}), f32[16,128,128]{2,1,0:T(8,128)}) %all-reduce.2.cloned.1.call-update) | async-done | bytes 1048592 | tf_op jit(solution)/shard_map/psum | solution.py:45
  (121 shorter events, 52.1 us)
Async XLA Ops:
  7.2 1.2 copy-start
  7.2 87.8 %all-gather.3.cloned.1.call-start = ((), (), s32[]{:S(2)}) async-start(), calls=%async_computation | async-start | bytes 10027008 | tf_op jit(solution)/shard_map/all_gather | solution.py:19
  7.9 5.0 copy-start.1
  7.9 184.5 %all-gather.5.cloned.1.call-start = ((), (), s32[]{:S(2)}) async-start(), calls=%async_computation.1 | async-start | bytes 17825792 | tf_op jit(solution)/shard_map/all_gather | solution.py:35
  12.8 586.0 %all-reduce.2.cloned.1.call-start = ((), (), s32[]{:S(2)}) async-start(), calls=%async_computation.2 | async-start | bytes 2097152 | tf_op jit(solution)/shard_map/psum | solution.py:45
Sparse Core Ops, SparseCore 0:
  10.4 84.5 all-gather.2
  96.8 95.5 all-gather.4
  489.3 109.5 all-reduce.1
where the time goes:
time: 609 us; the launch traced here: 607 us
  waiting for transfers between devices  286 us (47%)
  local copies, waits for them, and re-layouts  120 us (20%)
  matrix products  120 us (20%)
  other arithmetic  67.3 us (11%)
  between operations  13.8 us (2%)
    dot_general x16, matrix products, one_slot(): jnp.einsum('akij,kjl->kail', picked, u_slot, precision=highest)  106 us
    psum x1, waiting for transfers between devices, body(): summed = lax.psum(partial_sum, 'row')  105 us
    all_gather x1, waiting for transfers between devices, body(): lax.all_gather(u_local, 'row', axis=0, tiled=True)  97.4 us
    gather x16, local copies, waits for them, and re-layouts, select_blocks(): return jnp.take(sigma_rows, slot_ids, axis=1)  97.1 us
    all_gather x1, waiting for transfers between devices, body(): sigma_rows = lax.all_gather(sigma_anc, 'col', axis=1, tiled=True)  82 us
    add x16, other arithmetic, one_slot(): u_rows = u_rows + match[:, :, None, None] * u_slot[:, None, :, :]  61.5 us
    squeeze x16, local copies, waits for them, and re-layouts, body(): lax.scan(one_slot, (empty, empty), (lax.all_gather(u_local, 'row', axis=0...  20.7 us
  transfers between devices with their start and end apart: 3, of which 3 were waited for; matrix products, arithmetic and copies ran while one was open for 1% of the time, Pallas kernels for 0%

commit v1 on v0

v1 whole, which is shorter than its diff:
```python
import functools

import jax
import jax.numpy as jnp
from jax import lax
from jax.experimental import pallas as pl
from jax.experimental.pallas import tpu as pltpu
from jax.sharding import PartitionSpec as P

high = lax.Precision.HIGH


def node_kernel(struct_ref, base_ref, sig_ref, u_ref, zoff_ref, part_ref, y_scr, part_scr):
    k = pl.program_id(0)
    slots = u_ref.shape[0]
    rows = sig_ref.shape[0]
    width = u_ref.shape[-1]
    base = base_ref[0]

    def slot_step(s, acc):
        b = struct_ref[k, s]
        lhs = sig_ref[:, b].reshape(rows * width, width)
        return acc + jnp.dot(lhs, u_ref[s, 0], precision=high, preferred_element_type=jnp.float32)

    acc = lax.fori_loop(0, slots, slot_step, jnp.zeros((rows * width, width), jnp.float32))
    y_scr[...] = acc.reshape(rows, width, width)
    part_scr[...] = jnp.zeros_like(part_scr)

    @pl.loop(0, slots)
    def _(s):
        a = struct_ref[k, s] - base

        @pl.when((a >= 0) & (a < rows))
        def _():
            ut = jnp.transpose(u_ref[s, 0])
            part_scr[...] += jnp.dot(ut, y_scr[a], precision=high, preferred_element_type=jnp.float32)

    part_ref[0] = part_scr[...]

    for j in range(rows):
        def count(s, c):
            return c + (struct_ref[k, s] == base + j).astype(jnp.int32)

        hits = lax.fori_loop(0, slots, count, jnp.int32(0))
        zoff_ref[0, j] = jnp.where(hits > 0, -y_scr[j], 0.0)


def node_call(struct, base, sigma_rows, u_all):
    slots, nodes, width, _ = u_all.shape
    rows = sigma_rows.shape[0]
    grid_spec = pltpu.PrefetchScalarGridSpec(
        num_scalar_prefetch=2,
        grid=(nodes,),
        in_specs=[
            pl.BlockSpec(memory_space=pltpu.VMEM),
            pl.BlockSpec((slots, 1, width, width), lambda k, st, bs: (0, k, 0, 0)),
        ],
        out_specs=[
            pl.BlockSpec((1, rows, width, width), lambda k, st, bs: (k, 0, 0, 0)),
            pl.BlockSpec((1, width, width), lambda k, st, bs: (k, 0, 0)),
        ],
        scratch_shapes=[
            pltpu.VMEM((rows, width, width), jnp.float32),
            pltpu.VMEM((width, width), jnp.float32),
        ],
    )
    flops = 2 * nodes * slots * rows * width ** 3 * 3
    return pl.pallas_call(
        node_kernel,
        grid_spec=grid_spec,
        out_shape=[
            jax.ShapeDtypeStruct((nodes, rows, width, width), jnp.float32),
            jax.ShapeDtypeStruct((nodes, width, width), jnp.float32),
        ],
        compiler_params=pltpu.CompilerParams(vmem_limit_bytes=48 * 1024 * 1024),
        cost_estimate=pl.CostEstimate(flops=flops, transcendentals=0,
                                      bytes_accessed=4 * (sigma_rows.size + u_all.size + 2 * nodes * rows * width * width)),
    )(struct, base, sigma_rows, u_all)


def body(sigma_anc, factor, diag_inv, struct):
    row_count = sigma_anc.shape[0]
    row_index = lax.axis_index("row")
    base = jnp.reshape(row_index * row_count, (1,)).astype(jnp.int32)
    sigma_rows = lax.all_gather(sigma_anc, "col", axis=1, tiled=True)
    u_local = jnp.einsum("kij,kjl->kil", factor[0], diag_inv, precision=high)
    u_all = lax.all_gather(u_local, "row", axis=0, tiled=False)
    z_off, partial_sum = node_call(struct, base, sigma_rows, u_all)
    summed = lax.psum_scatter(partial_sum, "row", scatter_dimension=0, tiled=True)
    inverse_share = lax.dynamic_slice_in_dim(diag_inv, row_index, 1, 0)
    inverse_part = jnp.einsum("kij,kil->kjl", inverse_share, inverse_share, precision=high)
    return (z_off, inverse_part + summed)


def solution(mesh):
    in_specs = (
        P("row", "col", None, None),
        P("row", "col", None, None),
        P("col", None, None),
        P("col", None),
    )
    out_specs = (P("col", "row", None, None), P(("col", "row"), None, None))
    return jax.shard_map(body, mesh=mesh, in_specs=in_specs, out_specs=out_specs, check_vma=False)
```

time: 609 us -> 342 us (0.56)
  local copies, waits for them, and re-layouts: 120 us -> 1.14 us
  matrix products: 120 us -> 4.51 us
  Pallas kernels: 0 us -> 81.6 us
  other arithmetic: 67.3 us -> 0 us
  waiting for transfers between devices: 286 us -> 238 us
    dot_general x19 -> x2, matrix products: 120 us -> 4.51 us  [the longest x1 2.79 us: body(): u_local = jnp.einsum('kij,kjl->kil', factor[0], diag_inv, precision=high)]
    psum x1 -> x0, waiting for transfers between devices: 105 us -> none  [body(): summed = lax.psum(partial_sum, 'row')]
    gather x16 -> x0, local copies, waits for them, and re-layouts: 97.1 us -> none  [select_blocks(): return jnp.take(sigma_rows, slot_ids, axis=1)]
    pallas_call x0 -> x1, Pallas kernels: none -> 81.6 us  [node_call(): pl.pallas_call(node_kernel, grid_spec=grid_spec, out_shape=[jax.ShapeDtyp...]
    add x33 -> x0, other arithmetic: 61.5 us -> none  [the longest x16 61.5 us: one_slot(): u_rows = u_rows + match[:, :, None, None] * u_slot[:, None, :, :]]
    reduce_scatter x0 -> x1, waiting for transfers between devices: none -> 55.7 us  [body(): lax.psum_scatter(partial_sum, 'row', scatter_dimension=0, tiled=True)]
    squeeze x16 -> x0, local copies, waits for them, and re-layouts: 20.7 us -> none  [body(): lax.scan(one_slot, (empty, empty), (lax.all_gather(u_local, 'row', axis=0...]
where the time goes in v1:
time: 342 us; the launch traced here: 339 us
  waiting for transfers between devices  238 us (70%)
  Pallas kernels  81.6 us (24%)
  between operations  13.8 us (4%)
  matrix products  4.51 us (1%)
    all_gather x1, waiting for transfers between devices, body(): u_all = lax.all_gather(u_local, 'row', axis=0, tiled=False)  98 us
    all_gather x1, waiting for transfers between devices, body(): sigma_rows = lax.all_gather(sigma_anc, 'col', axis=1, tiled=True)  83.7 us
    pallas_call x1, Pallas kernels, node_call(): pl.pallas_call(node_kernel, grid_spec=grid_spec, out_shape=[jax.ShapeDtyp...  81.6 us
    reduce_scatter x1, waiting for transfers between devices, body(): lax.psum_scatter(partial_sum, 'row', scatter_dimension=0, tiled=True)  55.7 us
  transfers between devices with their start and end apart: 3, of which 3 were waited for; matrix products, arithmetic and copies ran while one was open for 1% of the time, Pallas kernels for 0%

profile of v1, /device:TPU:1, one launch (start us, length us, event | category | flops | bytes accessed | tf_op | source)
XLA Modules:
  0.0 339.3 jit_solution(6335259532995301431)
XLA Ops:
  7.2 0.0 copy-start
  7.2 0.0 all-gather.4.cloned.1.call-start
  7.2 0.7 all-gather.4.cloned.1.call-update
  7.9 0.0 all-gather.6.cloned.1.call-start
  8.0 0.4 copy-done
  8.4 2.8 fusion.1
  11.2 0.0 all-gather.6.cloned.1.call-update
  11.2 0.0 reduce-scatter.2.cloned.1.call-start
  11.3 83.7 %all-gather.4.cloned.1.call-done.sig_ref = f32[3,48,128,128]{3,2,1,0:T(8,128)} async-done(((f32[3,3,128,128]{3,2,1,0:T(8,128)}), f32[3,48,128,128]{3,2,1,0:T(8,128)}) %all-gather.4.cloned.1.call-update) | async-done | bytes 9437200 | tf_op jit(solution)/shard_map/all_gather | solution.py:85
  95.0 98.0 %all-gather.6.cloned.1.call-done = f32[256,128,128]{2,1,0:T(8,128)} async-done(((f32[16,128,128]{2,1,0:T(8,128)}), f32[256,128,128]{2,1,0:T(8,128)}) %all-gather.6.cloned.1.call-update) | async-done | bytes 16777232 | tf_op jit(solution)/shard_map/all_gather | solution.py:87
  193.0 0.0 copy-start.1
  193.0 0.7 copy-done.1
  193.7 81.6 %shard_map.59 = (f32[16,3,128,128]{3,2,1,0:T(8,128)}, f32[16,128,128]{2,1,0:T(8,128)}) custom-call(s32[16,16]{1,0:T(8,128)S(1)} %copy-done.1, s32[1]{0:T(128)} %bitcast.base_ref, f32[3,48,128,128]{3,2,1,0:T(8,128)} %all-gather.4.cloned.1.call-done.sig_ref, f32[16,16,128,128]{3,2,1,0:T(8,128)} %bitcast.13), custom_call_target="tpu_custom_call" | custom-call | flops 9663676416 | bytes 32505856 | tf_op jit(solution)/shard_map/pallas_call | solution.py:68
  275.3 0.0 reduce-scatter.2.cloned.1.call-update
  275.4 55.7 %reduce-scatter.2.cloned.1.call-done = f32[1,128,128]{2,1,0:T(8,128)} async-done(((f32[16,128,128]{2,1,0:T(8,128)}), f32[1,128,128]{2,1,0:T(8,128)}) %reduce-scatter.2.cloned.1.call-update) | async-done | bytes 65552 | tf_op jit(solution)/shard_map/reduce_scatter | solution.py:89
  331.1 1.7 fusion
Async XLA Ops:
  7.2 1.2 copy-start
  7.2 87.8 %all-gather.4.cloned.1.call-start = ((), (), s32[]{:S(2)}) async-start(), calls=%async_computation.1 | async-start | bytes 10027008 | tf_op jit(solution)/shard_map/all_gather | solution.py:85
  7.9 185.1 %all-gather.6.cloned.1.call-start = ((), (), s32[]{:S(2)}) async-start(), calls=%async_computation.3 | async-start | bytes 17825792 | tf_op jit(solution)/shard_map/all_gather | solution.py:87
  11.2 319.8 %reduce-scatter.2.cloned.1.call-start = ((), (), s32[]{:S(2)}) async-start(), calls=%async_computation.2 | async-start | bytes 1114112 | tf_op jit(solution)/shard_map/reduce_scatter | solution.py:89
  193.0 0.7 copy-start.1
Sparse Core Ops, SparseCore 0:
  10.4 84.5 all-gather.3
  97.4 95.5 all-gather.5
  275.5 55.5 reduce-scatter.1

commit v2 on v1

--- a/solution.py
+++ b/solution.py
@@ -78,15 +78,81 @@
     )(struct, base, sigma_rows, u_all)
 
 
+def ring_kernel(u_ref, out_ref, copy_sem, send_sem, recv_sem):
+    n = out_ref.shape[0]
+    half = n // 2
+    me = lax.axis_index("row")
+    col = lax.axis_index("col")
+    right = lax.rem(me + 1, n)
+    left = lax.rem(me + n - 1, n)
+
+    own = pltpu.make_async_copy(u_ref, out_ref.at[me], copy_sem.at[0])
+    own.start()
+
+    barrier = pltpu.get_barrier_semaphore()
+    for peer in (left, right):
+        pl.semaphore_signal(barrier, inc=1, device_id=(peer, col), device_id_type=pl.DeviceIdType.MESH)
+    pl.semaphore_wait(barrier, 2)
+    own.wait()
+
+    def link(step, direction):
+        if direction == 0:
+            slot = lax.rem(me - (step - 1) + n, n)
+            peer = right
+        else:
+            slot = lax.rem(me + (step - 1), n)
+            peer = left
+        return pltpu.make_async_remote_copy(
+            src_ref=out_ref.at[slot],
+            dst_ref=out_ref.at[slot],
+            send_sem=send_sem.at[direction, step - 1],
+            recv_sem=recv_sem.at[direction, step - 1],
+            device_id=(peer, col),
+            device_id_type=pl.DeviceIdType.MESH,
+        )
+
+    started = []
+    for step in range(1, half + 1):
+        directions = (0, 1) if step < half else (0,)
+        if step > 1:
+            for direction in (0, 1):
+                link(step - 1, direction).wait_recv()
+        for direction in directions:
+            copy = link(step, direction)
+            copy.start()
+            started.append(copy)
+    link(half, 0).wait_recv()
+    for copy in started:
+        copy.wait_send()
+
+
+def ring_gather(u_local, slots):
+    nodes, width, _ = u_local.shape
+    half = slots // 2
+    return pl.pallas_call(
+        ring_kernel,
+        out_shape=jax.ShapeDtypeStruct((slots, nodes, width, width), jnp.float32),
+        in_specs=[pl.BlockSpec(memory_space=pl.ANY)],
+        out_specs=pl.BlockSpec(memory_space=pl.ANY),
+        scratch_shapes=[
+            pltpu.SemaphoreType.DMA((1,)),
+            pltpu.SemaphoreType.DMA((2, half)),
+            pltpu.SemaphoreType.DMA((2, half)),
+        ],
+        compiler_params=pltpu.CompilerParams(collective_id=0, has_side_effects=True),
+    )(u_local)
+
+
 def body(sigma_anc, factor, diag_inv, struct):
     row_count = sigma_anc.shape[0]
     row_index = lax.axis_index("row")
     base = jnp.reshape(row_index * row_count, (1,)).astype(jnp.int32)
     sigma_rows = lax.all_gather(sigma_anc, "col", axis=1, tiled=True)
     u_local = jnp.einsum("kij,kjl->kil", factor[0], diag_inv, precision=high)
-    u_all = lax.all_gather(u_local, "row", axis=0, tiled=False)
+    u_all = ring_gather(u_local, lax.axis_size("row"))
     z_off, partial_sum = node_call(struct, base, sigma_rows, u_all)
-    summed = lax.psum_scatter(partial_sum, "row", scatter_dimension=0, tiled=True)
+    pieces = lax.all_to_all(partial_sum, "row", 0, 0, tiled=True)
+    summed = jnp.sum(pieces, axis=0, keepdims=True)
     inverse_share = lax.dynamic_slice_in_dim(diag_inv, row_index, 1, 0)
     inverse_part = jnp.einsum("kij,kil->kjl", inverse_share, inverse_share, precision=high)
     return (z_off, inverse_part + summed)

time: 342 us -> 287 us (0.84)
  waiting for transfers between devices: 238 us -> 28.6 us
  Pallas kernels: 81.6 us -> 226 us
  starting transfers between devices: 0.12 us -> 13.3 us
    pallas_call x0 -> x1, Pallas kernels: none -> 144 us  [ring_gather(): pl.pallas_call(ring_kernel, out_shape=jax.ShapeDtypeStruct((slots, nodes,...]
    all_gather x1 -> x0, waiting for transfers between devices: 98 us -> none  [body(): u_all = lax.all_gather(u_local, 'row', axis=0, tiled=False)]
    all_gather x1, waiting for transfers between devices: 83.7 us -> 0.02 us  [body(): sigma_rows = lax.all_gather(sigma_anc, 'col', axis=1, tiled=True)]
    reduce_scatter x1 -> x0, waiting for transfers between devices: 55.7 us -> none  [body(): lax.psum_scatter(partial_sum, 'row', scatter_dimension=0, tiled=True)]
    all_to_all x0 -> x1, waiting for transfers between devices: none -> 27.9 us  [body(): pieces = lax.all_to_all(partial_sum, 'row', 0, 0, tiled=True)]
    all_to_all x0 -> x1, starting transfers between devices: none -> 13.3 us  [body(): pieces = lax.all_to_all(partial_sum, 'row', 0, 0, tiled=True)]
  transfers between devices with their start and end apart: 3 -> 2, of which waited for: 3 -> 1; matrix products, arithmetic and copies ran while one was open for 1% -> 1% of each run, Pallas kernels for 0% -> 50%
where the time goes in v2:
time: 287 us; the launch traced here: 286 us
  Pallas kernels  226 us (79%)
  waiting for transfers between devices  28.6 us (10%)
  between operations  14.1 us (5%)
  starting transfers between devices  13.3 us (5%)
  matrix products  3.68 us (1%)
    pallas_call x1, Pallas kernels, ring_gather(): pl.pallas_call(ring_kernel, out_shape=jax.ShapeDtypeStruct((slots, nodes,...  144 us
    pallas_call x1, Pallas kernels, node_call(): pl.pallas_call(node_kernel, grid_spec=grid_spec, out_shape=[jax.ShapeDtyp...  81.4 us
    all_to_all x1, waiting for transfers between devices, body(): pieces = lax.all_to_all(partial_sum, 'row', 0, 0, tiled=True)  27.9 us
    all_to_all x1, starting transfers between devices, body(): pieces = lax.all_to_all(partial_sum, 'row', 0, 0, tiled=True)  13.3 us
  transfers between devices with their start and end apart: 2, of which 1 were waited for; matrix products, arithmetic and copies ran while one was open for 1% of the time, Pallas kernels for 50%

profile of v2, /device:TPU:1, one launch (start us, length us, event | category | flops | bytes accessed | tf_op | source)
XLA Modules:
  0.0 285.9 jit_solution(15821902673502678901)
XLA Ops:
  7.2 0.0 copy-start
  7.2 0.0 all-gather.2.cloned.1.call-start
  7.2 0.7 all-gather.2.cloned.1.call-update
  7.9 0.5 copy-done
  8.4 2.8 fusion.1.u_ref
  11.2 0.0 copy-start.1
  11.2 144.2 %shard_map.59.u_ref = f32[16,16,128,128]{3,2,1,0:T(8,128)} custom-call(f32[16,128,128]{2,1,0:T(8,128)} %fusion.1.u_ref), custom_call_target="tpu_custom_call" | custom-call | tf_op jit(solution)/shard_map/pallas_call | solution.py:132
  155.4 0.0 all-gather.2.cloned.1.call-done.sig_ref
  155.5 0.0 copy-done.1
  155.5 81.4 %shard_map.60 = (f32[16,3,128,128]{3,2,1,0:T(8,128)}, f32[16,128,128]{2,1,0:T(8,128)}) custom-call(s32[16,16]{1,0:T(8,128)S(1)} %copy-done.1, s32[1]{0:T(128)} %bitcast.base_ref, f32[3,48,128,128]{3,2,1,0:T(8,128)} %all-gather.2.cloned.1.call-done.sig_ref, f32[16,16,128,128]{3,2,1,0:T(8,128)} %shard_map.59.u_ref), custom_call_target="tpu_custom_call" | custom-call | flops 9663676416 | bytes 32505856 | tf_op jit(solution)/shard_map/pallas_call | solution.py:68
  236.9 13.3 %all-to-all-start = ((f32[16,128,128]{2,1,0:T(8,128)}), f32[16,128,128]{2,1,0:T(8,128)S(1)}, u32[]{:S(2)}, u32[]{:S(2)}) async-start(f32[16,128,128]{2,1,0:T(8,128)} %get-tuple-element.5), calls=%async_computation | async-start | bytes 2097152 | tf_op jit(solution)/shard_map/all_to_all | solution.py:154
  250.1 27.9 %all-to-all-done = f32[16,128,128]{2,1,0:T(8,128)S(1)} async-done(((f32[16,128,128]{2,1,0:T(8,128)}), f32[16,128,128]{2,1,0:T(8,128)S(1)}, u32[]{:S(2)}, u32[]{:S(2)}) %all-to-all-start) | async-done | bytes 1048608 | tf_op jit(solution)/shard_map/all_to_all | solution.py:154
  278.1 0.1 reduce_sum.9
  278.1 0.9 fusion
Async XLA Ops:
  7.2 1.2 copy-start
  7.2 148.3 %all-gather.2.cloned.1.call-start = ((), (), s32[]{:S(2)}) async-start(), calls=%async_computation.1 | async-start | bytes 10027008 | tf_op jit(solution)/shard_map/all_gather | solution.py:150
  11.2 144.3 %copy-start.1 = (s32[16,16]{1,0:T(8,128)S(1)}, s32[16,16]{1,0:T(8,128)}, u32[]{:S(2)}) copy-start(s32[16,16]{1,0:T(8,128)} %struct_ref.1) | copy-start | bytes 3076
  236.9 41.2 %all-to-all-start = ((f32[16,128,128]{2,1,0:T(8,128)}), f32[16,128,128]{2,1,0:T(8,128)S(1)}, u32[]{:S(2)}, u32[]{:S(2)}) async-start(f32[16,128,128]{2,1,0:T(8,128)} %get-tuple-element.5), calls=%async_computation | async-start | bytes 2097152 | tf_op jit(solution)/shard_map/all_to_all | solution.py:154
Sparse Core Ops, SparseCore 0:
  10.4 84.5 all-gather.1

commit v3 on v2

--- a/solution.py
+++ b/solution.py
@@ -17,12 +17,16 @@
     width = u_ref.shape[-1]
     base = base_ref[0]
 
-    def slot_step(s, acc):
-        b = struct_ref[k, s]
-        lhs = sig_ref[:, b].reshape(rows * width, width)
-        return acc + jnp.dot(lhs, u_ref[s, 0], precision=high, preferred_element_type=jnp.float32)
+    def slot_pair(i, acc):
+        first = 2 * i
+        second = first + 1
+        lhs = jnp.concatenate(
+            [sig_ref[:, struct_ref[k, first]].reshape(rows * width, width),
+             sig_ref[:, struct_ref[k, second]].reshape(rows * width, width)], axis=1)
+        rhs = jnp.concatenate([u_ref[first, 0], u_ref[second, 0]], axis=0)
+        return acc + jnp.dot(lhs, rhs, precision=high, preferred_element_type=jnp.float32)
 
-    acc = lax.fori_loop(0, slots, slot_step, jnp.zeros((rows * width, width), jnp.float32))
+    acc = lax.fori_loop(0, slots // 2, slot_pair, jnp.zeros((rows * width, width), jnp.float32))
     y_scr[...] = acc.reshape(rows, width, width)
     part_scr[...] = jnp.zeros_like(part_scr)
 
@@ -78,9 +82,10 @@
     )(struct, base, sigma_rows, u_all)
 
 
-def ring_kernel(u_ref, out_ref, copy_sem, send_sem, recv_sem):
+def ring_kernel(parts, u_ref, out_ref, copy_sem, send_sem, recv_sem):
     n = out_ref.shape[0]
     half = n // 2
+    chunk = out_ref.shape[1] // parts
     me = lax.axis_index("row")
     col = lax.axis_index("col")
     right = lax.rem(me + 1, n)
@@ -95,18 +100,19 @@
     pl.semaphore_wait(barrier, 2)
     own.wait()
 
-    def link(step, direction):
+    def link(step, direction, part):
         if direction == 0:
             slot = lax.rem(me - (step - 1) + n, n)
             peer = right
         else:
             slot = lax.rem(me + (step - 1), n)
             peer = left
+        piece = pl.ds(part * chunk, chunk)
         return pltpu.make_async_remote_copy(
-            src_ref=out_ref.at[slot],
-            dst_ref=out_ref.at[slot],
-            send_sem=send_sem.at[direction, step - 1],
-            recv_sem=recv_sem.at[direction, step - 1],
+            src_ref=out_ref.at[slot, piece],
+            dst_ref=out_ref.at[slot, piece],
+            send_sem=send_sem.at[direction, step - 1, part],
+            recv_sem=recv_sem.at[direction, step - 1, part],
             device_id=(peer, col),
             device_id_type=pl.DeviceIdType.MESH,
         )
@@ -114,30 +120,32 @@
     started = []
     for step in range(1, half + 1):
         directions = (0, 1) if step < half else (0,)
-        if step > 1:
-            for direction in (0, 1):
-                link(step - 1, direction).wait_recv()
         for direction in directions:
-            copy = link(step, direction)
-            copy.start()
-            started.append(copy)
-    link(half, 0).wait_recv()
+            for part in range(parts):
+                if step > 1:
+                    link(step - 1, direction, part).wait_recv()
+                copy = link(step, direction, part)
+                copy.start()
+                started.append(copy)
+    for part in range(parts):
+        link(half, 0, part).wait_recv()
+        link(half - 1, 1, part).wait_recv()
     for copy in started:
         copy.wait_send()
 
 
-def ring_gather(u_local, slots):
+def ring_gather(u_local, slots, parts=4):
     nodes, width, _ = u_local.shape
     half = slots // 2
     return pl.pallas_call(
-        ring_kernel,
+        functools.partial(ring_kernel, parts),
         out_shape=jax.ShapeDtypeStruct((slots, nodes, width, width), jnp.float32),
         in_specs=[pl.BlockSpec(memory_space=pl.ANY)],
         out_specs=pl.BlockSpec(memory_space=pl.ANY),
         scratch_shapes=[
             pltpu.SemaphoreType.DMA((1,)),
-            pltpu.SemaphoreType.DMA((2, half)),
-            pltpu.SemaphoreType.DMA((2, half)),
+            pltpu.SemaphoreType.DMA((2, half, parts)),
+            pltpu.SemaphoreType.DMA((2, half, parts)),
         ],
         compiler_params=pltpu.CompilerParams(collective_id=0, has_side_effects=True),
     )(u_local)

time: 287 us -> 248 us (0.86)
  Pallas kernels: 226 us -> 190 us
  starting transfers between devices: 13.3 us -> 10.2 us
    pallas_call x1, Pallas kernels: 144 us -> 125 us  [ring_gather(): pl.pallas_call(functools.partial(ring_kernel, parts), out_shape=jax.Shape...]
    pallas_call x1, Pallas kernels: 81.4 us -> 65.2 us  [node_call(): pl.pallas_call(node_kernel, grid_spec=grid_spec, out_shape=[jax.ShapeDtyp...]
    all_to_all x1, starting transfers between devices: 13.3 us -> 10.1 us  [body(): pieces = lax.all_to_all(partial_sum, 'row', 0, 0, tiled=True)]
where the time goes in v3:
time: 248 us; the launch traced here: 247 us
  Pallas kernels  190 us (77%)
  waiting for transfers between devices  28.6 us (12%)
  between operations  14.1 us (6%)
  starting transfers between devices  10.2 us (4%)
  matrix products  3.68 us (1%)
    pallas_call x1, Pallas kernels, ring_gather(): pl.pallas_call(functools.partial(ring_kernel, parts), out_shape=jax.Shape...  125 us
    pallas_call x1, Pallas kernels, node_call(): pl.pallas_call(node_kernel, grid_spec=grid_spec, out_shape=[jax.ShapeDtyp...  65.2 us
    all_to_all x1, waiting for transfers between devices, body(): pieces = lax.all_to_all(partial_sum, 'row', 0, 0, tiled=True)  27.9 us
    all_to_all x1, starting transfers between devices, body(): pieces = lax.all_to_all(partial_sum, 'row', 0, 0, tiled=True)  10.1 us
  transfers between devices with their start and end apart: 2, of which 1 were waited for; matrix products, arithmetic and copies ran while one was open for 1% of the time, Pallas kernels for 50%

profile of v3, /device:TPU:1, one launch (start us, length us, event | category | flops | bytes accessed | tf_op | source)
XLA Modules:
  0.0 247.0 jit_solution(1821524545674121140)
XLA Ops:
  7.2 0.0 copy-start
  7.2 0.0 all-gather.2.cloned.1.call-start
  7.2 0.7 all-gather.2.cloned.1.call-update
  7.9 0.5 copy-done
  8.4 2.8 %fusion.1.u_ref = f32[16,128,128]{2,1,0:T(8,128)} fusion(f32[16,128,128]{2,1,0:T(8,128)S(1)} %copy-done, f32[1,16,128,128]{3,2,1,0:T(8,128)} %param.5), kind=kOutput, calls=%fused_computation.2 | convolution fusion | flops 201326592 | bytes 3145728 | tf_op jit(solution)/shard_map/kij,kjl->kil/dot_general | solution.py:159
  11.2 0.0 copy-start.1
  11.2 124.7 %shard_map.59.u_ref = f32[16,16,128,128]{3,2,1,0:T(8,128)} custom-call(f32[16,128,128]{2,1,0:T(8,128)} %fusion.1.u_ref), custom_call_target="tpu_custom_call" | custom-call | tf_op jit(solution)/shard_map/pallas_call | solution.py:140
  135.9 0.0 all-gather.2.cloned.1.call-done.sig_ref
  136.0 0.0 copy-done.1
  136.0 65.2 %shard_map.60 = (f32[16,3,128,128]{3,2,1,0:T(8,128)}, f32[16,128,128]{2,1,0:T(8,128)}) custom-call(s32[16,16]{1,0:T(8,128)S(1)} %copy-done.1, s32[1]{0:T(128)} %bitcast.base_ref, f32[3,48,128,128]{3,2,1,0:T(8,128)} %all-gather.2.cloned.1.call-done.sig_ref, f32[16,16,128,128]{3,2,1,0:T(8,128)} %shard_map.59.u_ref), custom_call_target="tpu_custom_call" | custom-call | flops 9663676416 | bytes 32505856 | tf_op jit(solution)/shard_map/pallas_call | solution.py:72
  201.1 10.1 %all-to-all-start = ((f32[16,128,128]{2,1,0:T(8,128)}), f32[16,128,128]{2,1,0:T(8,128)S(1)}, u32[]{:S(2)}, u32[]{:S(2)}) async-start(f32[16,128,128]{2,1,0:T(8,128)} %get-tuple-element.5), calls=%async_computation | async-start | bytes 2097152 | tf_op jit(solution)/shard_map/all_to_all | solution.py:162
  211.3 27.9 %all-to-all-done = f32[16,128,128]{2,1,0:T(8,128)S(1)} async-done(((f32[16,128,128]{2,1,0:T(8,128)}), f32[16,128,128]{2,1,0:T(8,128)S(1)}, u32[]{:S(2)}, u32[]{:S(2)}) %all-to-all-start) | async-done | bytes 1048608 | tf_op jit(solution)/shard_map/all_to_all | solution.py:162
  239.2 0.1 reduce_sum.9
  239.3 0.9 fusion
Async XLA Ops:
  7.2 1.2 copy-start
  7.2 128.8 %all-gather.2.cloned.1.call-start = ((), (), s32[]{:S(2)}) async-start(), calls=%async_computation.1 | async-start | bytes 10027008 | tf_op jit(solution)/shard_map/all_gather | solution.py:158
  11.2 124.8 %copy-start.1 = (s32[16,16]{1,0:T(8,128)S(1)}, s32[16,16]{1,0:T(8,128)}, u32[]{:S(2)}) copy-start(s32[16,16]{1,0:T(8,128)} %struct_ref.1) | copy-start | bytes 3076
  201.1 38.1 %all-to-all-start = ((f32[16,128,128]{2,1,0:T(8,128)}), f32[16,128,128]{2,1,0:T(8,128)S(1)}, u32[]{:S(2)}, u32[]{:S(2)}) async-start(f32[16,128,128]{2,1,0:T(8,128)} %get-tuple-element.5), calls=%async_computation | async-start | bytes 2097152 | tf_op jit(solution)/shard_map/all_to_all | solution.py:162
Sparse Core Ops, SparseCore 0:
  10.4 84.5 all-gather.1

commit v4 on v3

--- a/solution.py
+++ b/solution.py
@@ -82,73 +82,227 @@
     )(struct, base, sigma_rows, u_all)
 
 
-def ring_kernel(parts, u_ref, out_ref, copy_sem, send_sem, recv_sem):
+def greet_neighbours(me, col, n):
+    barrier = pltpu.get_barrier_semaphore()
+    for peer in (lax.rem(me + n - 1, n), lax.rem(me + 1, n)):
+        pl.semaphore_signal(barrier, inc=1, device_id=(peer, col), device_id_type=pl.DeviceIdType.MESH)
+    pl.semaphore_wait(barrier, 2)
+
+
+def step_parts(step, direction, half, parts):
+    if step < half:
+        return range(parts)
+    if direction == 0:
+        return range(parts // 2)
+    return range(parts // 2, parts)
+
+
+def ring_kernel(steps, parts, u_ref, out_ref, copy_sem, send_sem, recv_sem):
     n = out_ref.shape[0]
-    half = n // 2
     chunk = out_ref.shape[1] // parts
     me = lax.axis_index("row")
     col = lax.axis_index("col")
-    right = lax.rem(me + 1, n)
-    left = lax.rem(me + n - 1, n)
-
-    own = pltpu.make_async_copy(u_ref, out_ref.at[me], copy_sem.at[0])
-    own.start()
-
-    barrier = pltpu.get_barrier_semaphore()
-    for peer in (left, right):
-        pl.semaphore_signal(barrier, inc=1, device_id=(peer, col), device_id_type=pl.DeviceIdType.MESH)
-    pl.semaphore_wait(barrier, 2)
-    own.wait()
 
     def link(step, direction, part):
         if direction == 0:
             slot = lax.rem(me - (step - 1) + n, n)
-            peer = right
+            peer = lax.rem(me + 1, n)
         else:
             slot = lax.rem(me + (step - 1), n)
-            peer = left
+            peer = lax.rem(me + n - 1, n)
         piece = pl.ds(part * chunk, chunk)
         return pltpu.make_async_remote_copy(
-            src_ref=out_ref.at[slot, piece],
-            dst_ref=out_ref.at[slot, piece],
+            src_ref=out_ref.at[slot, piece], dst_ref=out_ref.at[slot, piece],
             send_sem=send_sem.at[direction, step - 1, part],
             recv_sem=recv_sem.at[direction, step - 1, part],
-            device_id=(peer, col),
-            device_id_type=pl.DeviceIdType.MESH,
-        )
+            device_id=(peer, col), device_id_type=pl.DeviceIdType.MESH)
+
+    own = pltpu.make_async_copy(u_ref, out_ref.at[me], copy_sem.at[0])
+    own.start()
+    greet_neighbours(me, col, n)
+    own.wait()
 
     started = []
-    for step in range(1, half + 1):
-        directions = (0, 1) if step < half else (0,)
-        for direction in directions:
+    for step in range(1, steps + 1):
+        for direction in (0, 1):
             for part in range(parts):
                 if step > 1:
                     link(step - 1, direction, part).wait_recv()
                 copy = link(step, direction, part)
                 copy.start()
                 started.append(copy)
-    for part in range(parts):
-        link(half, 0, part).wait_recv()
-        link(half - 1, 1, part).wait_recv()
+    for direction in (0, 1):
+        for part in range(parts):
+            link(steps, direction, part).wait_recv()
     for copy in started:
         copy.wait_send()
 
 
-def ring_gather(u_local, slots, parts=4):
+def ring_gather(u_local, slots, steps, parts):
     nodes, width, _ = u_local.shape
-    half = slots // 2
     return pl.pallas_call(
-        functools.partial(ring_kernel, parts),
+        functools.partial(ring_kernel, steps, parts),
         out_shape=jax.ShapeDtypeStruct((slots, nodes, width, width), jnp.float32),
         in_specs=[pl.BlockSpec(memory_space=pl.ANY)],
         out_specs=pl.BlockSpec(memory_space=pl.ANY),
         scratch_shapes=[
             pltpu.SemaphoreType.DMA((1,)),
-            pltpu.SemaphoreType.DMA((2, half, parts)),
-            pltpu.SemaphoreType.DMA((2, half, parts)),
+            pltpu.SemaphoreType.DMA((2, steps, parts)),
+            pltpu.SemaphoreType.DMA((2, steps, parts)),
         ],
         compiler_params=pltpu.CompilerParams(collective_id=0, has_side_effects=True),
     )(u_local)
+
+
+def fused_kernel(first, parts, struct_ref, base_ref, sig_ref, u_in, u_out, zoff_ref, part_ref,
+                 u_vmem, y_acc, load_sem, send_sem, recv_sem):
+    n = u_out.shape[0]
+    half = n // 2
+    nodes = u_out.shape[1]
+    chunk = nodes // parts
+    rows = sig_ref.shape[0]
+    width = sig_ref.shape[-1]
+    me = lax.axis_index("row")
+    col = lax.axis_index("col")
+    base = base_ref[0]
+
+    def link(step, direction, part):
+        if direction == 0:
+            slot = lax.rem(me - (step - 1) + n, n)
+            peer = lax.rem(me + 1, n)
+        else:
+            slot = lax.rem(me + (step - 1), n)
+            peer = lax.rem(me + n - 1, n)
+        piece = pl.ds(part * chunk, chunk)
+        return pltpu.make_async_remote_copy(
+            src_ref=u_out.at[slot, piece], dst_ref=u_out.at[slot, piece],
+            send_sem=send_sem.at[direction, step - 1 - first, part],
+            recv_sem=recv_sem.at[direction, step - 1 - first, part],
+            device_id=(peer, col), device_id_type=pl.DeviceIdType.MESH)
+
+    def load(slot):
+        return pltpu.make_async_copy(u_out.at[slot], u_vmem.at[slot], load_sem.at[slot])
+
+    def wrap(offset):
+        return lax.rem(me + offset + 2 * n, n)
+
+    greet_neighbours(me, col, n)
+    for offset in range(-first, first + 1):
+        load(wrap(offset)).start()
+
+    started = []
+
+    def send_step(step):
+        for direction in (0, 1):
+            for part in step_parts(step, direction, half, parts):
+                copy = link(step, direction, part)
+                copy.start()
+                started.append(copy)
+
+    send_step(first + 1)
+
+    def lhs_block(k, slot):
+        return sig_ref[:, struct_ref[k, slot]].reshape(rows * width, width)
+
+    def add_single(slot):
+        def node(k, carry):
+            y_acc[k] += jnp.dot(lhs_block(k, slot), u_vmem[slot, k], precision=high,
+                                preferred_element_type=jnp.float32)
+            return carry
+        lax.fori_loop(0, nodes, node, 0)
+
+    def add_pair(one, two):
+        def node(k, carry):
+            lhs = jnp.concatenate([lhs_block(k, one), lhs_block(k, two)], axis=1)
+            rhs = jnp.concatenate([u_vmem[one, k], u_vmem[two, k]], axis=0)
+            y_acc[k] += jnp.dot(lhs, rhs, precision=high, preferred_element_type=jnp.float32)
+            return carry
+        lax.fori_loop(0, nodes, node, 0)
+
+    load(me).wait()
+    y_acc[...] = jnp.zeros_like(y_acc)
+    add_single(me)
+    for offset in range(1, first + 1):
+        load(wrap(-offset)).wait()
+        load(wrap(offset)).wait()
+        add_pair(wrap(-offset), wrap(offset))
+
+    for step in range(first + 1, half + 1):
+        for direction in (0, 1):
+            for part in step_parts(step, direction, half, parts):
+                link(step, direction, part).wait_recv()
+        if step < half:
+            send_step(step + 1)
+            one, two = wrap(-step), wrap(step)
+            load(one).start()
+            load(two).start()
+            load(one).wait()
+            load(two).wait()
+            add_pair(one, two)
+        else:
+            last = wrap(half)
+            load(last).start()
+            load(last).wait()
+            add_single(last)
+
+    for copy in started:
+        copy.wait_send()
+
+    def finish(k, carry):
+        y = y_acc[k].reshape(rows, width, width)
+        total = jnp.zeros((width, width), jnp.float32)
+        for j in range(rows):
+            def scan(s, acc):
+                hit = (struct_ref[k, s] == base + j).astype(jnp.int32)
+                return acc[0] + hit, acc[1] + hit * s
+            hits, slot = lax.fori_loop(0, n, scan, (jnp.int32(0), jnp.int32(0)))
+            slot = jnp.minimum(slot, n - 1)
+            term = jnp.dot(jnp.transpose(u_vmem[slot, k]), y[j], precision=high,
+                           preferred_element_type=jnp.float32)
+            total = total + jnp.where(hits > 0, term, 0.0)
+            zoff_ref[k, j] = jnp.where(hits > 0, -y[j], 0.0)
+        part_ref[k] = total
+        return carry
+
+    lax.fori_loop(0, nodes, finish, 0)
+
+
+def fused_call(struct, base, sigma_rows, u_all, first, parts):
+    slots, nodes, width, _ = u_all.shape
+    rows = sigma_rows.shape[0]
+    later = slots // 2 - first
+    flops = 2 * nodes * slots * rows * width ** 3 * 3
+    return pl.pallas_call(
+        functools.partial(fused_kernel, first, parts),
+        out_shape=[
+            jax.ShapeDtypeStruct(u_all.shape, jnp.float32),
+            jax.ShapeDtypeStruct((nodes, rows, width, width), jnp.float32),
+            jax.ShapeDtypeStruct((nodes, width, width), jnp.float32),
+        ],
+        in_specs=[
+            pl.BlockSpec(memory_space=pltpu.SMEM),
+            pl.BlockSpec(memory_space=pltpu.SMEM),
+            pl.BlockSpec(memory_space=pltpu.VMEM),
+            pl.BlockSpec(memory_space=pl.ANY),
+        ],
+        out_specs=[
+            pl.BlockSpec(memory_space=pl.ANY),
+            pl.BlockSpec(memory_space=pltpu.VMEM),
+            pl.BlockSpec(memory_space=pltpu.VMEM),
+        ],
+        scratch_shapes=[
+            pltpu.VMEM(u_all.shape, jnp.float32),
+            pltpu.VMEM((nodes, rows * width, width), jnp.float32),
+            pltpu.SemaphoreType.DMA((slots,)),
+            pltpu.SemaphoreType.DMA((2, later, parts)),
+            pltpu.SemaphoreType.DMA((2, later, parts)),
+        ],
+        input_output_aliases={3: 0},
+        compiler_params=pltpu.CompilerParams(collective_id=1, has_side_effects=True,
+                                             vmem_limit_bytes=60 * 1024 * 1024),
+        cost_estimate=pl.CostEstimate(flops=flops, transcendentals=0,
+                                      bytes_accessed=4 * (sigma_rows.size + u_all.size)),
+    )(struct, base, sigma_rows, u_all)
 
 
 def body(sigma_anc, factor, diag_inv, struct):
@@ -157,8 +311,9 @@
     base = jnp.reshape(row_index * row_count, (1,)).astype(jnp.int32)
     sigma_rows = lax.all_gather(sigma_anc, "col", axis=1, tiled=True)
     u_local = jnp.einsum("kij,kjl->kil", factor[0], diag_inv, precision=high)
-    u_all = ring_gather(u_local, lax.axis_size("row"))
-    z_off, partial_sum = node_call(struct, base, sigma_rows, u_all)
+    first, parts = 5, 4
+    u_head = ring_gather(u_local, lax.axis_size("row"), first, parts)
+    unused_u, z_off, partial_sum = fused_call(struct, base, sigma_rows, u_head, first, parts)
     pieces = lax.all_to_all(partial_sum, "row", 0, 0, tiled=True)
     summed = jnp.sum(pieces, axis=0, keepdims=True)
     inverse_share = lax.dynamic_slice_in_dim(diag_inv, row_index, 1, 0)

time: 248 us -> 246 us (level)
  local copies, waits for them, and re-layouts: 0.49 us -> 4.39 us
  starting transfers between devices: 10.2 us -> 7.61 us
    unnamed x4 -> x3, local copies, waits for them, and re-layouts: 0.49 us -> 4.39 us
    all_to_all x1, starting transfers between devices: 10.1 us -> 7.57 us  [body(): pieces = lax.all_to_all(partial_sum, 'row', 0, 0, tiled=True)]
  transfers between devices with their start and end apart: 2 -> 2, of which waited for: 1 -> 1; matrix products, arithmetic and copies ran while one was open for 1% -> 1% of each run, Pallas kernels for 50% -> 39%
where the time goes in v4:
time: 246 us
  Pallas kernels  188 us (76%)
  waiting for transfers between devices  28.7 us (12%)
  between operations  14.1 us (6%)
  starting transfers between devices  7.61 us (3%)
  local copies, waits for them, and re-layouts  4.39 us (2%)
  matrix products  3.68 us (1%)
    pallas_call x1, Pallas kernels, ring_gather(): pl.pallas_call(functools.partial(ring_kernel, steps, parts), out_shape=ja...  95 us
    pallas_call x1, Pallas kernels, fused_call(): pl.pallas_call(functools.partial(fused_kernel, first, parts), out_shape=[...  92.6 us
    all_to_all x1, waiting for transfers between devices, body(): pieces = lax.all_to_all(partial_sum, 'row', 0, 0, tiled=True)  28 us
    all_to_all x1, starting transfers between devices, body(): pieces = lax.all_to_all(partial_sum, 'row', 0, 0, tiled=True)  7.57 us
  transfers between devices with their start and end apart: 2, of which 1 were waited for; matrix products, arithmetic and copies ran while one was open for 1% of the time, Pallas kernels for 39%

profile of v4, /device:TPU:1, one launch (start us, length us, event | category | flops | bytes accessed | tf_op | source)
XLA Modules:
  0.0 246.1 jit_solution(15207753909066186040)
XLA Ops:
  7.2 0.0 copy-start
  7.2 0.0 all-gather.2.cloned.1.call-start
  7.2 0.7 all-gather.2.cloned.1.call-update
  7.9 0.5 copy-done
  8.4 2.8 %fusion.1.u_ref = f32[16,128,128]{2,1,0:T(8,128)} fusion(f32[16,128,128]{2,1,0:T(8,128)S(1)} %copy-done, f32[1,16,128,128]{3,2,1,0:T(8,128)} %param.5), kind=kOutput, calls=%fused_computation.2 | convolution fusion | flops 201326592 | bytes 3145728 | tf_op jit(solution)/shard_map/kij,kjl->kil/dot_general | solution.py:313
  11.2 95.0 %shard_map.59.u_in = f32[16,16,128,128]{3,2,1,0:T(8,128)} custom-call(f32[16,128,128]{2,1,0:T(8,128)} %fusion.1.u_ref), custom_call_target="tpu_custom_call" | custom-call | tf_op jit(solution)/shard_map/pallas_call | solution.py:143
  106.2 0.0 all-gather.2.cloned.1.call-done.sig_ref
  106.2 92.6 %shard_map.60 = (f32[16,16,128,128]{3,2,1,0:T(8,128)}, f32[16,3,128,128]{3,2,1,0:T(8,128)}, f32[16,128,128]{2,1,0:T(8,128)}) custom-call(s32[16,16]{1,0:T(8,128)} %struct_ref.1, s32[1]{0:T(128)} %bitcast.base_ref, f32[3,48,128,128]{3,2,1,0:T(8,128)} %all-gather.2.cloned.1.call-done.sig_ref, ...), custom_call_target="tpu_custom_call", output_to_operand_aliasing={{0}: (3, {})} | custom-call | flops 9663676416 | bytes 26214400 | tf_op jit(solution)/shard_map/pallas_call | solution.py:275
  198.8 7.6 %all-to-all-start = ((f32[16,128,128]{2,1,0:T(8,128)}), f32[16,128,128]{2,1,0:T(8,128)S(1)}, u32[]{:S(2)}, u32[]{:S(2)}) async-start(f32[16,128,128]{2,1,0:T(8,128)} %get-tuple-element.5), calls=%async_computation | async-start | bytes 2097152 | tf_op jit(solution)/shard_map/all_to_all | solution.py:317
  206.4 28.0 %all-to-all-done = f32[16,128,128]{2,1,0:T(8,128)S(1)} async-done(((f32[16,128,128]{2,1,0:T(8,128)}), f32[16,128,128]{2,1,0:T(8,128)S(1)}, u32[]{:S(2)}, u32[]{:S(2)}) %all-to-all-start) | async-done | bytes 1048608 | tf_op jit(solution)/shard_map/all_to_all | solution.py:317
  234.4 0.1 reduce_sum.9
  234.4 0.9 fusion
  235.3 3.9 %copy.9 = f32[16,3,128,128]{3,2,1,0:T(8,128)} copy(f32[16,3,128,128]{3,2,1,0:T(8,128)} %get-tuple-element.8) | data formatting | bytes 6291456
Async XLA Ops:
  7.2 1.2 copy-start
  7.2 99.0 %all-gather.2.cloned.1.call-start = ((), (), s32[]{:S(2)}) async-start(), calls=%async_computation.1 | async-start | bytes 10027008 | tf_op jit(solution)/shard_map/all_gather | solution.py:312
  198.8 35.5 %all-to-all-start = ((f32[16,128,128]{2,1,0:T(8,128)}), f32[16,128,128]{2,1,0:T(8,128)S(1)}, u32[]{:S(2)}, u32[]{:S(2)}) async-start(f32[16,128,128]{2,1,0:T(8,128)} %get-tuple-element.5), calls=%async_computation | async-start | bytes 2097152 | tf_op jit(solution)/shard_map/all_to_all | solution.py:317
Sparse Core Ops, SparseCore 0:
  10.4 84.5 all-gather.1

commit v5 on v4

--- a/solution.py
+++ b/solution.py
@@ -311,7 +311,7 @@
     base = jnp.reshape(row_index * row_count, (1,)).astype(jnp.int32)
     sigma_rows = lax.all_gather(sigma_anc, "col", axis=1, tiled=True)
     u_local = jnp.einsum("kij,kjl->kil", factor[0], diag_inv, precision=high)
-    first, parts = 5, 4
+    first, parts = 3, 4
     u_head = ring_gather(u_local, lax.axis_size("row"), first, parts)
     unused_u, z_off, partial_sum = fused_call(struct, base, sigma_rows, u_head, first, parts)
     pieces = lax.all_to_all(partial_sum, "row", 0, 0, tiled=True)

time: 246 us -> 250 us (1.016)
  waiting for transfers between devices: 28.7 us -> 40.2 us
  Pallas kernels: 188 us -> 179 us
    pallas_call x1, Pallas kernels: 95 us -> 72.2 us  [ring_gather(): pl.pallas_call(functools.partial(ring_kernel, steps, parts), out_shape=ja...]
    pallas_call x1, Pallas kernels: 92.6 us -> 106 us  [fused_call(): pl.pallas_call(functools.partial(fused_kernel, first, parts), out_shape=[...]
    all_gather x1, waiting for transfers between devices: 0.02 us -> 11.6 us  [body(): sigma_rows = lax.all_gather(sigma_anc, 'col', axis=1, tiled=True)]
  transfers between devices with their start and end apart: 2 -> 2, of which waited for: 1 -> 2; matrix products, arithmetic and copies ran while one was open for 1% -> 1% of each run, Pallas kernels for 39% -> 29%
where the time goes in v5:
time: 250 us; the launch traced here: 249 us
  Pallas kernels  179 us (72%)
  waiting for transfers between devices  40.2 us (16%)
  between operations  14.1 us (6%)
  starting transfers between devices  8.03 us (3%)
  local copies, waits for them, and re-layouts  4.39 us (2%)
  matrix products  3.68 us (1%)
    pallas_call x1, Pallas kernels, fused_call(): pl.pallas_call(functools.partial(fused_kernel, first, parts), out_shape=[...  106 us
    pallas_call x1, Pallas kernels, ring_gather(): pl.pallas_call(functools.partial(ring_kernel, steps, parts), out_shape=ja...  72.2 us
    all_to_all x1, waiting for transfers between devices, body(): pieces = lax.all_to_all(partial_sum, 'row', 0, 0, tiled=True)  27.9 us
    all_gather x1, waiting for transfers between devices, body(): sigma_rows = lax.all_gather(sigma_anc, 'col', axis=1, tiled=True)  11.6 us
    all_to_all x1, starting transfers between devices, body(): pieces = lax.all_to_all(partial_sum, 'row', 0, 0, tiled=True)  7.99 us
  transfers between devices with their start and end apart: 2, of which 2 were waited for; matrix products, arithmetic and copies ran while one was open for 1% of the time, Pallas kernels for 29%

profile of v5, /device:TPU:1, one launch (start us, length us, event | category | flops | bytes accessed | tf_op | source)
XLA Modules:
  0.0 249.1 jit_solution(1196516361220975703)
XLA Ops:
  7.2 0.0 copy-start
  7.2 0.0 all-gather.2.cloned.1.call-start
  7.2 0.7 all-gather.2.cloned.1.call-update
  7.9 0.5 copy-done
  8.4 2.8 %fusion.1.u_ref = f32[16,128,128]{2,1,0:T(8,128)} fusion(f32[16,128,128]{2,1,0:T(8,128)S(1)} %copy-done, f32[1,16,128,128]{3,2,1,0:T(8,128)} %param.5), kind=kOutput, calls=%fused_computation.2 | convolution fusion | flops 201326592 | bytes 3145728 | tf_op jit(solution)/shard_map/kij,kjl->kil/dot_general | solution.py:313
  11.2 72.2 %shard_map.59.u_in = f32[16,16,128,128]{3,2,1,0:T(8,128)} custom-call(f32[16,128,128]{2,1,0:T(8,128)} %fusion.1.u_ref), custom_call_target="tpu_custom_call" | custom-call | tf_op jit(solution)/shard_map/pallas_call | solution.py:143
  83.4 11.6 %all-gather.2.cloned.1.call-done.sig_ref = f32[3,48,128,128]{3,2,1,0:T(8,128)} async-done(((f32[3,3,128,128]{3,2,1,0:T(8,128)}), f32[3,48,128,128]{3,2,1,0:T(8,128)}) %all-gather.2.cloned.1.call-update) | async-done | bytes 9437200 | tf_op jit(solution)/shard_map/all_gather | solution.py:312
  95.0 106.5 %shard_map.60 = (f32[16,16,128,128]{3,2,1,0:T(8,128)}, f32[16,3,128,128]{3,2,1,0:T(8,128)}, f32[16,128,128]{2,1,0:T(8,128)}) custom-call(s32[16,16]{1,0:T(8,128)} %struct_ref.1, s32[1]{0:T(128)} %bitcast.base_ref, f32[3,48,128,128]{3,2,1,0:T(8,128)} %all-gather.2.cloned.1.call-done.sig_ref, ...), custom_call_target="tpu_custom_call", output_to_operand_aliasing={{0}: (3, {})} | custom-call | flops 9663676416 | bytes 26214400 | tf_op jit(solution)/shard_map/pallas_call | solution.py:275
  201.5 8.0 %all-to-all-start = ((f32[16,128,128]{2,1,0:T(8,128)}), f32[16,128,128]{2,1,0:T(8,128)S(1)}, u32[]{:S(2)}, u32[]{:S(2)}) async-start(f32[16,128,128]{2,1,0:T(8,128)} %get-tuple-element.5), calls=%async_computation | async-start | bytes 2097152 | tf_op jit(solution)/shard_map/all_to_all | solution.py:317
  209.5 27.9 %all-to-all-done = f32[16,128,128]{2,1,0:T(8,128)S(1)} async-done(((f32[16,128,128]{2,1,0:T(8,128)}), f32[16,128,128]{2,1,0:T(8,128)S(1)}, u32[]{:S(2)}, u32[]{:S(2)}) %all-to-all-start) | async-done | bytes 1048608 | tf_op jit(solution)/shard_map/all_to_all | solution.py:317
  237.4 0.1 reduce_sum.9
  237.5 0.9 fusion
  238.4 3.9 %copy.9 = f32[16,3,128,128]{3,2,1,0:T(8,128)} copy(f32[16,3,128,128]{3,2,1,0:T(8,128)} %get-tuple-element.8) | data formatting | bytes 6291456
Async XLA Ops:
  7.2 1.2 copy-start
  7.2 87.8 %all-gather.2.cloned.1.call-start = ((), (), s32[]{:S(2)}) async-start(), calls=%async_computation.1 | async-start | bytes 10027008 | tf_op jit(solution)/shard_map/all_gather | solution.py:312
  201.5 35.9 %all-to-all-start = ((f32[16,128,128]{2,1,0:T(8,128)}), f32[16,128,128]{2,1,0:T(8,128)S(1)}, u32[]{:S(2)}, u32[]{:S(2)}) async-start(f32[16,128,128]{2,1,0:T(8,128)} %get-tuple-element.5), calls=%async_computation | async-start | bytes 2097152 | tf_op jit(solution)/shard_map/all_to_all | solution.py:317
Sparse Core Ops, SparseCore 0:
  10.4 84.5 all-gather.1

commit v6 on v4

--- a/solution.py
+++ b/solution.py
@@ -154,8 +154,8 @@
     )(u_local)
 
 
-def fused_kernel(first, parts, struct_ref, base_ref, sig_ref, u_in, u_out, zoff_ref, part_ref,
-                 u_vmem, y_acc, load_sem, send_sem, recv_sem):
+def fused_kernel(first, parts, struct_ref, base_ref, sig_ref, u_in, u_out, zoff_ref, sum_ref,
+                 u_vmem, y_acc, part_ref, gather_buf, load_sem, send_sem, recv_sem, out_sem, in_sem):
     n = u_out.shape[0]
     half = n // 2
     nodes = u_out.shape[1]
@@ -186,7 +186,11 @@
     def wrap(offset):
         return lax.rem(me + offset + 2 * n, n)
 
-    greet_neighbours(me, col, n)
+    barrier = pltpu.get_barrier_semaphore()
+    for offset in range(1, n):
+        pl.semaphore_signal(barrier, inc=1, device_id=(lax.rem(me + offset, n), col),
+                            device_id_type=pl.DeviceIdType.MESH)
+    pl.semaphore_wait(barrier, n - 1)
     for offset in range(-first, first + 1):
         load(wrap(offset)).start()
 
@@ -266,6 +270,20 @@
 
     lax.fori_loop(0, nodes, finish, 0)
 
+    def share(offset):
+        return pltpu.make_async_remote_copy(
+            src_ref=part_ref.at[lax.rem(me + offset, n)], dst_ref=gather_buf.at[me],
+            send_sem=out_sem.at[offset], recv_sem=in_sem.at[offset],
+            device_id=(lax.rem(me + offset, n), col), device_id_type=pl.DeviceIdType.MESH)
+
+    for offset in range(1, n):
+        share(offset).start()
+    gather_buf[me] = part_ref[me]
+    for offset in range(1, n):
+        share(offset).wait_send()
+        share(offset).wait_recv()
+    sum_ref[0] = jnp.sum(gather_buf[...], axis=0)
+
 
 def fused_call(struct, base, sigma_rows, u_all, first, parts):
     slots, nodes, width, _ = u_all.shape
@@ -277,7 +295,7 @@
         out_shape=[
             jax.ShapeDtypeStruct(u_all.shape, jnp.float32),
             jax.ShapeDtypeStruct((nodes, rows, width, width), jnp.float32),
-            jax.ShapeDtypeStruct((nodes, width, width), jnp.float32),
+            jax.ShapeDtypeStruct((1, width, width), jnp.float32),
         ],
         in_specs=[
             pl.BlockSpec(memory_space=pltpu.SMEM),
@@ -293,9 +311,13 @@
         scratch_shapes=[
             pltpu.VMEM(u_all.shape, jnp.float32),
             pltpu.VMEM((nodes, rows * width, width), jnp.float32),
+            pltpu.VMEM((nodes, width, width), jnp.float32),
+            pltpu.VMEM((slots, width, width), jnp.float32),
             pltpu.SemaphoreType.DMA((slots,)),
             pltpu.SemaphoreType.DMA((2, later, parts)),
             pltpu.SemaphoreType.DMA((2, later, parts)),
+            pltpu.SemaphoreType.DMA((slots,)),
+            pltpu.SemaphoreType.DMA((slots,)),
         ],
         input_output_aliases={3: 0},
         compiler_params=pltpu.CompilerParams(collective_id=1, has_side_effects=True,
@@ -313,9 +335,7 @@
     u_local = jnp.einsum("kij,kjl->kil", factor[0], diag_inv, precision=high)
     first, parts = 5, 4
     u_head = ring_gather(u_local, lax.axis_size("row"), first, parts)
-    unused_u, z_off, partial_sum = fused_call(struct, base, sigma_rows, u_head, first, parts)
-    pieces = lax.all_to_all(partial_sum, "row", 0, 0, tiled=True)
-    summed = jnp.sum(pieces, axis=0, keepdims=True)
+    unused_u, z_off, summed = fused_call(struct, base, sigma_rows, u_head, first, parts)
     inverse_share = lax.dynamic_slice_in_dim(diag_inv, row_index, 1, 0)
     inverse_part = jnp.einsum("kij,kil->kjl", inverse_share, inverse_share, precision=high)
     return (z_off, inverse_part + summed)

time: 246 us -> 239 us (0.972)
  waiting for transfers between devices: 28.7 us -> 0.7 us
  Pallas kernels: 188 us -> 215 us
  starting transfers between devices: 7.61 us -> 0.04 us
    all_to_all x1 -> x0, waiting for transfers between devices: 28 us -> none  [body(): pieces = lax.all_to_all(partial_sum, 'row', 0, 0, tiled=True)]
    pallas_call x1, Pallas kernels: 92.6 us -> 120 us  [fused_call(): pl.pallas_call(functools.partial(fused_kernel, first, parts), out_shape=[...]
    all_to_all x1 -> x0, starting transfers between devices: 7.57 us -> none  [body(): pieces = lax.all_to_all(partial_sum, 'row', 0, 0, tiled=True)]
  transfers between devices with their start and end apart: 2 -> 1, of which waited for: 1 -> 0; matrix products, arithmetic and copies ran while one was open for 1% -> 1% of each run, Pallas kernels for 39% -> 40%
where the time goes in v6:
time: 239 us
  Pallas kernels  215 us (90%)
  between operations  14.1 us (6%)
  matrix products  4.52 us (2%)
  local copies, waits for them, and re-layouts  4.39 us (2%)
    pallas_call x1, Pallas kernels, fused_call(): pl.pallas_call(functools.partial(fused_kernel, first, parts), out_shape=[...  120 us
    pallas_call x1, Pallas kernels, ring_gather(): pl.pallas_call(functools.partial(ring_kernel, steps, parts), out_shape=ja...  95 us
  transfers between devices with their start and end apart: 1, of which 0 were waited for; matrix products, arithmetic and copies ran while one was open for 1% of the time, Pallas kernels for 40%

profile of v6, /device:TPU:1, one launch (start us, length us, event | category | flops | bytes accessed | tf_op | source)
XLA Modules:
  0.0 238.6 jit_solution(13250274772081330036)
XLA Ops:
  7.2 0.0 copy-start
  7.2 0.0 all-gather.2.cloned.1.call-start
  7.2 0.7 all-gather.2.cloned.1.call-update
  7.9 0.5 copy-done
  8.4 2.8 %fusion.1.u_ref = f32[16,128,128]{2,1,0:T(8,128)} fusion(f32[16,128,128]{2,1,0:T(8,128)S(1)} %copy-done, f32[1,16,128,128]{3,2,1,0:T(8,128)} %param.5), kind=kOutput, calls=%fused_computation.2 | convolution fusion | flops 201326592 | bytes 3145728 | tf_op jit(solution)/shard_map/kij,kjl->kil/dot_general | solution.py:335
  11.2 95.0 %shard_map.59.u_in = f32[16,16,128,128]{3,2,1,0:T(8,128)} custom-call(f32[16,128,128]{2,1,0:T(8,128)} %fusion.1.u_ref), custom_call_target="tpu_custom_call" | custom-call | tf_op jit(solution)/shard_map/pallas_call | solution.py:143
  106.2 0.0 all-gather.2.cloned.1.call-done.sig_ref
  106.2 119.9 %shard_map.60 = (f32[16,16,128,128]{3,2,1,0:T(8,128)}, f32[16,3,128,128]{3,2,1,0:T(8,128)}, f32[1,128,128]{2,1,0:T(8,128)}) custom-call(s32[16,16]{1,0:T(8,128)} %struct_ref.1, s32[1]{0:T(128)} %bitcast.base_ref, f32[3,48,128,128]{3,2,1,0:T(8,128)} %all-gather.2.cloned.1.call-done.sig_ref, ...), custom_call_target="tpu_custom_call", output_to_operand_aliasing={{0}: (3, {})} | custom-call | flops 9663676416 | bytes 26214400 | tf_op jit(solution)/shard_map/pallas_call | solution.py:293
  226.1 1.7 fusion
  227.8 3.9 %copy.9 = f32[16,3,128,128]{3,2,1,0:T(8,128)} copy(f32[16,3,128,128]{3,2,1,0:T(8,128)} %get-tuple-element.8) | data formatting | bytes 6291456
Async XLA Ops:
  7.2 1.2 copy-start
  7.2 99.0 %all-gather.2.cloned.1.call-start = ((), (), s32[]{:S(2)}) async-start(), calls=%async_computation | async-start | bytes 10027008 | tf_op jit(solution)/shard_map/all_gather | solution.py:334
Sparse Core Ops, SparseCore 0:
  10.4 84.5 all-gather.1

commit v7 on v6

--- a/solution.py
+++ b/solution.py
@@ -223,6 +223,29 @@
             return carry
         lax.fori_loop(0, nodes, node, 0)
 
+    def ring_event(step):
+        for direction in (0, 1):
+            for part in step_parts(step, direction, half, parts):
+                link(step, direction, part).wait_recv()
+        if step < half:
+            send_step(step + 1)
+            load(wrap(-step)).start()
+            load(wrap(step)).start()
+        else:
+            load(wrap(half)).start()
+
+    def arrived(step):
+        if step < half:
+            one, two = wrap(-step), wrap(step)
+            load(one).wait()
+            load(two).wait()
+            add_pair(one, two)
+        else:
+            last = wrap(half)
+            load(last).wait()
+            add_single(last)
+
+    processed = first
     load(me).wait()
     y_acc[...] = jnp.zeros_like(y_acc)
     add_single(me)
@@ -230,27 +253,32 @@
         load(wrap(-offset)).wait()
         load(wrap(offset)).wait()
         add_pair(wrap(-offset), wrap(offset))
-
-    for step in range(first + 1, half + 1):
-        for direction in (0, 1):
-            for part in step_parts(step, direction, half, parts):
-                link(step, direction, part).wait_recv()
-        if step < half:
-            send_step(step + 1)
-            one, two = wrap(-step), wrap(step)
-            load(one).start()
-            load(two).start()
-            load(one).wait()
-            load(two).wait()
-            add_pair(one, two)
-        else:
-            last = wrap(half)
-            load(last).start()
-            load(last).wait()
-            add_single(last)
+        if offset % 2 == 0 and processed < half:
+            processed += 1
+            ring_event(processed)
+    done = first + 1
+    while done <= half:
+        if done <= processed:
+            arrived(done)
+            done += 1
+        else:
+            processed += 1
+            ring_event(processed)
 
     for copy in started:
         copy.wait_send()
+
+    def share_to(k):
+        return pltpu.make_async_remote_copy(
+            src_ref=part_ref.at[k], dst_ref=gather_buf.at[me],
+            send_sem=out_sem.at[k], recv_sem=in_sem.at[me],
+            device_id=(k, col), device_id_type=pl.DeviceIdType.MESH)
+
+    def share_from(j):
+        return pltpu.make_async_remote_copy(
+            src_ref=part_ref.at[j], dst_ref=gather_buf.at[j],
+            send_sem=out_sem.at[j], recv_sem=in_sem.at[j],
+            device_id=(j, col), device_id_type=pl.DeviceIdType.MESH)
 
     def finish(k, carry):
         y = y_acc[k].reshape(rows, width, width)
@@ -266,22 +294,26 @@
             total = total + jnp.where(hits > 0, term, 0.0)
             zoff_ref[k, j] = jnp.where(hits > 0, -y[j], 0.0)
         part_ref[k] = total
+
+        @pl.when((k >= 1) & (k - 1 != me))
+        def _():
+            share_to(k - 1).start()
+
         return carry
 
     lax.fori_loop(0, nodes, finish, 0)
 
-    def share(offset):
-        return pltpu.make_async_remote_copy(
-            src_ref=part_ref.at[lax.rem(me + offset, n)], dst_ref=gather_buf.at[me],
-            send_sem=out_sem.at[offset], recv_sem=in_sem.at[offset],
-            device_id=(lax.rem(me + offset, n), col), device_id_type=pl.DeviceIdType.MESH)
-
-    for offset in range(1, n):
-        share(offset).start()
+    @pl.when(me != nodes - 1)
+    def _():
+        share_to(nodes - 1).start()
+
     gather_buf[me] = part_ref[me]
-    for offset in range(1, n):
-        share(offset).wait_send()
-        share(offset).wait_recv()
+    for j in range(n):
+        @pl.when(me != j)
+        def _():
+            share_to(j).wait_send()
+            share_from(j).wait_recv()
+
     sum_ref[0] = jnp.sum(gather_buf[...], axis=0)
 
 

time: 239 us -> 224 us (0.937)
  Pallas kernels: 215 us -> 200 us
    pallas_call x1, Pallas kernels: 120 us -> 105 us  [fused_call(): pl.pallas_call(functools.partial(fused_kernel, first, parts), out_shape=[...]
  transfers between devices with their start and end apart: 1 -> 1, of which waited for: 0 -> 0; matrix products, arithmetic and copies ran while one was open for 1% -> 1% of each run, Pallas kernels for 40% -> 42%
where the time goes in v7:
time: 224 us
  Pallas kernels  200 us (89%)
  between operations  14.1 us (6%)
  matrix products  4.52 us (2%)
  local copies, waits for them, and re-layouts  4.39 us (2%)
    pallas_call x1, Pallas kernels, fused_call(): pl.pallas_call(functools.partial(fused_kernel, first, parts), out_shape=[...  105 us
    pallas_call x1, Pallas kernels, ring_gather(): pl.pallas_call(functools.partial(ring_kernel, steps, parts), out_shape=ja...  95 us
  transfers between devices with their start and end apart: 1, of which 0 were waited for; matrix products, arithmetic and copies ran while one was open for 1% of the time, Pallas kernels for 42%

profile of v7, /device:TPU:1, one launch (start us, length us, event | category | flops | bytes accessed | tf_op | source)
XLA Modules:
  0.0 223.7 jit_solution(10600822789284054063)
XLA Ops:
  7.2 0.0 copy-start
  7.2 0.0 all-gather.2.cloned.1.call-start
  7.2 0.7 all-gather.2.cloned.1.call-update
  7.9 0.5 copy-done
  8.4 2.8 %fusion.1.u_ref = f32[16,128,128]{2,1,0:T(8,128)} fusion(f32[16,128,128]{2,1,0:T(8,128)S(1)} %copy-done, f32[1,16,128,128]{3,2,1,0:T(8,128)} %param.5), kind=kOutput, calls=%fused_computation.2 | convolution fusion | flops 201326592 | bytes 3145728 | tf_op jit(solution)/shard_map/kij,kjl->kil/dot_general | solution.py:367
  11.2 95.0 %shard_map.59.u_in = f32[16,16,128,128]{3,2,1,0:T(8,128)} custom-call(f32[16,128,128]{2,1,0:T(8,128)} %fusion.1.u_ref), custom_call_target="tpu_custom_call" | custom-call | tf_op jit(solution)/shard_map/pallas_call | solution.py:143
  106.2 0.0 all-gather.2.cloned.1.call-done.sig_ref
  106.2 105.0 %shard_map.60 = (f32[16,16,128,128]{3,2,1,0:T(8,128)}, f32[16,3,128,128]{3,2,1,0:T(8,128)}, f32[1,128,128]{2,1,0:T(8,128)}) custom-call(s32[16,16]{1,0:T(8,128)} %struct_ref.1, s32[1]{0:T(128)} %bitcast.base_ref, f32[3,48,128,128]{3,2,1,0:T(8,128)} %all-gather.2.cloned.1.call-done.sig_ref, ...), custom_call_target="tpu_custom_call", output_to_operand_aliasing={{0}: (3, {})} | custom-call | flops 9663676416 | bytes 26214400 | tf_op jit(solution)/shard_map/pallas_call | solution.py:325
  211.3 1.7 fusion
  213.0 3.9 %copy.9 = f32[16,3,128,128]{3,2,1,0:T(8,128)} copy(f32[16,3,128,128]{3,2,1,0:T(8,128)} %get-tuple-element.8) | data formatting | bytes 6291456
Async XLA Ops:
  7.2 1.2 copy-start
  7.2 99.0 %all-gather.2.cloned.1.call-start = ((), (), s32[]{:S(2)}) async-start(), calls=%async_computation | async-start | bytes 10027008 | tf_op jit(solution)/shard_map/all_gather | solution.py:366
Sparse Core Ops, SparseCore 0:
  10.4 84.5 all-gather.1

commit v8 on v7

--- a/solution.py
+++ b/solution.py
@@ -365,7 +365,7 @@
     base = jnp.reshape(row_index * row_count, (1,)).astype(jnp.int32)
     sigma_rows = lax.all_gather(sigma_anc, "col", axis=1, tiled=True)
     u_local = jnp.einsum("kij,kjl->kil", factor[0], diag_inv, precision=high)
-    first, parts = 5, 4
+    first, parts = 4, 4
     u_head = ring_gather(u_local, lax.axis_size("row"), first, parts)
     unused_u, z_off, summed = fused_call(struct, base, sigma_rows, u_head, first, parts)
     inverse_share = lax.dynamic_slice_in_dim(diag_inv, row_index, 1, 0)

time: 224 us -> 218 us (0.973)
  Pallas kernels: 200 us -> 194 us
    pallas_call x1, Pallas kernels: 95 us -> 83.6 us  [ring_gather(): pl.pallas_call(functools.partial(ring_kernel, steps, parts), out_shape=ja...]
    pallas_call x1, Pallas kernels: 105 us -> 111 us  [fused_call(): pl.pallas_call(functools.partial(fused_kernel, first, parts), out_shape=[...]
  transfers between devices with their start and end apart: 1 -> 1, of which waited for: 0 -> 1; matrix products, arithmetic and copies ran while one was open for 1% -> 1% of each run, Pallas kernels for 42% -> 38%
where the time goes in v8:
time: 218 us
  Pallas kernels  194 us (89%)
  between operations  14.1 us (6%)
  matrix products  4.52 us (2%)
  local copies, waits for them, and re-layouts  4.39 us (2%)
    pallas_call x1, Pallas kernels, fused_call(): pl.pallas_call(functools.partial(fused_kernel, first, parts), out_shape=[...  111 us
    pallas_call x1, Pallas kernels, ring_gather(): pl.pallas_call(functools.partial(ring_kernel, steps, parts), out_shape=ja...  83.6 us
    unnamed x3, local copies, waits for them, and re-layouts  4.39 us
  transfers between devices with their start and end apart: 1, of which 1 were waited for; matrix products, arithmetic and copies ran while one was open for 1% of the time, Pallas kernels for 38%

profile of v8, /device:TPU:1, one launch (start us, length us, event | category | flops | bytes accessed | tf_op | source)
XLA Modules:
  0.0 218.1 jit_solution(5789111644626671810)
XLA Ops:
  7.2 0.0 copy-start
  7.2 0.0 all-gather.2.cloned.1.call-start
  7.2 0.7 all-gather.2.cloned.1.call-update
  7.9 0.5 copy-done
  8.4 2.8 %fusion.1.u_ref = f32[16,128,128]{2,1,0:T(8,128)} fusion(f32[16,128,128]{2,1,0:T(8,128)S(1)} %copy-done, f32[1,16,128,128]{3,2,1,0:T(8,128)} %param.5), kind=kOutput, calls=%fused_computation.2 | convolution fusion | flops 201326592 | bytes 3145728 | tf_op jit(solution)/shard_map/kij,kjl->kil/dot_general | solution.py:367
  11.2 83.6 %shard_map.59.u_in = f32[16,16,128,128]{3,2,1,0:T(8,128)} custom-call(f32[16,128,128]{2,1,0:T(8,128)} %fusion.1.u_ref), custom_call_target="tpu_custom_call" | custom-call | tf_op jit(solution)/shard_map/pallas_call | solution.py:143
  94.8 0.2 all-gather.2.cloned.1.call-done.sig_ref
  95.0 110.6 %shard_map.60 = (f32[16,16,128,128]{3,2,1,0:T(8,128)}, f32[16,3,128,128]{3,2,1,0:T(8,128)}, f32[1,128,128]{2,1,0:T(8,128)}) custom-call(s32[16,16]{1,0:T(8,128)} %struct_ref.1, s32[1]{0:T(128)} %bitcast.base_ref, f32[3,48,128,128]{3,2,1,0:T(8,128)} %all-gather.2.cloned.1.call-done.sig_ref, ...), custom_call_target="tpu_custom_call", output_to_operand_aliasing={{0}: (3, {})} | custom-call | flops 9663676416 | bytes 26214400 | tf_op jit(solution)/shard_map/pallas_call | solution.py:325
  205.6 1.7 fusion
  207.4 3.9 %copy.9 = f32[16,3,128,128]{3,2,1,0:T(8,128)} copy(f32[16,3,128,128]{3,2,1,0:T(8,128)} %get-tuple-element.8) | data formatting | bytes 6291456
Async XLA Ops:
  7.2 1.2 copy-start
  7.2 87.8 %all-gather.2.cloned.1.call-start = ((), (), s32[]{:S(2)}) async-start(), calls=%async_computation | async-start | bytes 10027008 | tf_op jit(solution)/shard_map/all_gather | solution.py:366
Sparse Core Ops, SparseCore 0:
  10.4 84.5 all-gather.1

commit v9 on v8

--- a/solution.py
+++ b/solution.py
@@ -8,78 +8,6 @@
 from jax.sharding import PartitionSpec as P
 
 high = lax.Precision.HIGH
-
-
-def node_kernel(struct_ref, base_ref, sig_ref, u_ref, zoff_ref, part_ref, y_scr, part_scr):
-    k = pl.program_id(0)
-    slots = u_ref.shape[0]
-    rows = sig_ref.shape[0]
-    width = u_ref.shape[-1]
-    base = base_ref[0]
-
-    def slot_pair(i, acc):
-        first = 2 * i
-        second = first + 1
-        lhs = jnp.concatenate(
-            [sig_ref[:, struct_ref[k, first]].reshape(rows * width, width),
-             sig_ref[:, struct_ref[k, second]].reshape(rows * width, width)], axis=1)
-        rhs = jnp.concatenate([u_ref[first, 0], u_ref[second, 0]], axis=0)
-        return acc + jnp.dot(lhs, rhs, precision=high, preferred_element_type=jnp.float32)
-
-    acc = lax.fori_loop(0, slots // 2, slot_pair, jnp.zeros((rows * width, width), jnp.float32))
-    y_scr[...] = acc.reshape(rows, width, width)
-    part_scr[...] = jnp.zeros_like(part_scr)
-
-    @pl.loop(0, slots)
-    def _(s):
-        a = struct_ref[k, s] - base
-
-        @pl.when((a >= 0) & (a < rows))
-        def _():
-            ut = jnp.transpose(u_ref[s, 0])
-            part_scr[...] += jnp.dot(ut, y_scr[a], precision=high, preferred_element_type=jnp.float32)
-
-    part_ref[0] = part_scr[...]
-
-    for j in range(rows):
-        def count(s, c):
-            return c + (struct_ref[k, s] == base + j).astype(jnp.int32)
-
-        hits = lax.fori_loop(0, slots, count, jnp.int32(0))
-        zoff_ref[0, j] = jnp.where(hits > 0, -y_scr[j], 0.0)
-
-
-def node_call(struct, base, sigma_rows, u_all):
-    slots, nodes, width, _ = u_all.shape
-    rows = sigma_rows.shape[0]
-    grid_spec = pltpu.PrefetchScalarGridSpec(
-        num_scalar_prefetch=2,
-        grid=(nodes,),
-        in_specs=[
-            pl.BlockSpec(memory_space=pltpu.VMEM),
-            pl.BlockSpec((slots, 1, width, width), lambda k, st, bs: (0, k, 0, 0)),
-        ],
-        out_specs=[
-            pl.BlockSpec((1, rows, width, width), lambda k, st, bs: (k, 0, 0, 0)),
-            pl.BlockSpec((1, width, width), lambda k, st, bs: (k, 0, 0)),
-        ],
-        scratch_shapes=[
-            pltpu.VMEM((rows, width, width), jnp.float32),
-            pltpu.VMEM((width, width), jnp.float32),
-        ],
-    )
-    flops = 2 * nodes * slots * rows * width ** 3 * 3
-    return pl.pallas_call(
-        node_kernel,
-        grid_spec=grid_spec,
-        out_shape=[
-            jax.ShapeDtypeStruct((nodes, rows, width, width), jnp.float32),
-            jax.ShapeDtypeStruct((nodes, width, width), jnp.float32),
-        ],
-        compiler_params=pltpu.CompilerParams(vmem_limit_bytes=48 * 1024 * 1024),
-        cost_estimate=pl.CostEstimate(flops=flops, transcendentals=0,
-                                      bytes_accessed=4 * (sigma_rows.size + u_all.size + 2 * nodes * rows * width * width)),
-    )(struct, base, sigma_rows, u_all)
 
 
 def greet_neighbours(me, col, n):
@@ -154,7 +82,7 @@
     )(u_local)
 
 
-def fused_kernel(first, parts, struct_ref, base_ref, sig_ref, u_in, u_out, zoff_ref, sum_ref,
+def fused_kernel(first, parts, struct_ref, hit_ref, slot_ref, sig_ref, u_in, u_out, zoff_ref, sum_ref,
                  u_vmem, y_acc, part_ref, gather_buf, load_sem, send_sem, recv_sem, out_sem, in_sem):
     n = u_out.shape[0]
     half = n // 2
@@ -164,7 +92,6 @@
     width = sig_ref.shape[-1]
     me = lax.axis_index("row")
     col = lax.axis_index("col")
-    base = base_ref[0]
 
     def link(step, direction, part):
         if direction == 0:
@@ -257,13 +184,18 @@
             processed += 1
             ring_event(processed)
     done = first + 1
-    while done <= half:
+    while done < half:
         if done <= processed:
             arrived(done)
             done += 1
         else:
             processed += 1
             ring_event(processed)
+    while processed < half:
+        processed += 1
+        ring_event(processed)
+    last = wrap(half)
+    load(last).wait()
 
     for copy in started:
         copy.wait_send()
@@ -281,14 +213,13 @@
             device_id=(j, col), device_id_type=pl.DeviceIdType.MESH)
 
     def finish(k, carry):
-        y = y_acc[k].reshape(rows, width, width)
+        y = y_acc[k] + jnp.dot(lhs_block(k, last), u_vmem[last, k], precision=high,
+                               preferred_element_type=jnp.float32)
+        y = y.reshape(rows, width, width)
         total = jnp.zeros((width, width), jnp.float32)
         for j in range(rows):
-            def scan(s, acc):
-                hit = (struct_ref[k, s] == base + j).astype(jnp.int32)
-                return acc[0] + hit, acc[1] + hit * s
-            hits, slot = lax.fori_loop(0, n, scan, (jnp.int32(0), jnp.int32(0)))
-            slot = jnp.minimum(slot, n - 1)
+            hits = hit_ref[k, j]
+            slot = jnp.minimum(slot_ref[k, j], n - 1)
             term = jnp.dot(jnp.transpose(u_vmem[slot, k]), y[j], precision=high,
                            preferred_element_type=jnp.float32)
             total = total + jnp.where(hits > 0, term, 0.0)
@@ -317,7 +248,7 @@
     sum_ref[0] = jnp.sum(gather_buf[...], axis=0)
 
 
-def fused_call(struct, base, sigma_rows, u_all, first, parts):
+def fused_call(struct, hit, slot, sigma_rows, u_all, first, parts):
     slots, nodes, width, _ = u_all.shape
     rows = sigma_rows.shape[0]
     later = slots // 2 - first
@@ -332,6 +263,7 @@
         in_specs=[
             pl.BlockSpec(memory_space=pltpu.SMEM),
             pl.BlockSpec(memory_space=pltpu.SMEM),
+            pl.BlockSpec(memory_space=pltpu.SMEM),
             pl.BlockSpec(memory_space=pltpu.VMEM),
             pl.BlockSpec(memory_space=pl.ANY),
         ],
@@ -351,23 +283,26 @@
             pltpu.SemaphoreType.DMA((slots,)),
             pltpu.SemaphoreType.DMA((slots,)),
         ],
-        input_output_aliases={3: 0},
+        input_output_aliases={4: 0},
         compiler_params=pltpu.CompilerParams(collective_id=1, has_side_effects=True,
                                              vmem_limit_bytes=60 * 1024 * 1024),
         cost_estimate=pl.CostEstimate(flops=flops, transcendentals=0,
                                       bytes_accessed=4 * (sigma_rows.size + u_all.size)),
-    )(struct, base, sigma_rows, u_all)
+    )(struct, hit, slot, sigma_rows, u_all)
 
 
 def body(sigma_anc, factor, diag_inv, struct):
     row_count = sigma_anc.shape[0]
     row_index = lax.axis_index("row")
-    base = jnp.reshape(row_index * row_count, (1,)).astype(jnp.int32)
     sigma_rows = lax.all_gather(sigma_anc, "col", axis=1, tiled=True)
     u_local = jnp.einsum("kij,kjl->kil", factor[0], diag_inv, precision=high)
     first, parts = 4, 4
     u_head = ring_gather(u_local, lax.axis_size("row"), first, parts)
-    unused_u, z_off, summed = fused_call(struct, base, sigma_rows, u_head, first, parts)
+    wanted = row_index * row_count + jnp.arange(row_count, dtype=jnp.int32)
+    match = struct[:, :, None] == wanted[None, None, :]
+    hit = jnp.any(match, axis=1).astype(jnp.int32)
+    slot = jnp.argmax(match, axis=1).astype(jnp.int32)
+    unused_u, z_off, summed = fused_call(struct, hit, slot, sigma_rows, u_head, first, parts)
     inverse_share = lax.dynamic_slice_in_dim(diag_inv, row_index, 1, 0)
     inverse_part = jnp.einsum("kij,kil->kjl", inverse_share, inverse_share, precision=high)
     return (z_off, inverse_part + summed)

time: 218 us -> 208 us (0.954)
  Pallas kernels: 194 us -> 180 us
  other arithmetic: 0 us -> 2.36 us
    pallas_call x1, Pallas kernels: 111 us -> 96.8 us  [fused_call(): pl.pallas_call(functools.partial(fused_kernel, first, parts), out_shape=[...]
  transfers between devices with their start and end apart: 1 -> 1, of which waited for: 1 -> 0; matrix products, arithmetic and copies ran while one was open for 1% -> 3% of each run, Pallas kernels for 38% -> 40%
where the time goes in v9:
time: 208 us; the launch traced here: 207 us
  Pallas kernels  180 us (87%)
  between operations  14.1 us (7%)
  local copies, waits for them, and re-layouts  5.27 us (3%)
  matrix products  4.52 us (2%)
  other arithmetic  2.36 us (1%)
    pallas_call x1, Pallas kernels, fused_call(): pl.pallas_call(functools.partial(fused_kernel, first, parts), out_shape=[...  96.8 us
    pallas_call x1, Pallas kernels, ring_gather(): pl.pallas_call(functools.partial(ring_kernel, steps, parts), out_shape=ja...  83.6 us
  transfers between devices with their start and end apart: 1, of which 0 were waited for; matrix products, arithmetic and copies ran while one was open for 3% of the time, Pallas kernels for 40%

profile of v9, /device:TPU:1, one launch (start us, length us, event | category | flops | bytes accessed | tf_op | source)
XLA Modules:
  0.0 207.3 jit_solution(16227132720485835407)
XLA Ops:
  7.2 0.0 copy-start
  7.2 0.0 all-gather.2.cloned.1.call-start
  7.2 0.7 all-gather.2.cloned.1.call-update
  7.9 0.9 compare_reduce_fusion.1
  8.9 1.4 compare_reduce_fusion
  10.3 0.7 copy.10.slot_ref
  11.0 0.7 copy.9.hit_ref
  11.6 0.0 copy-done
  11.6 2.8 %fusion.1.u_ref = f32[16,128,128]{2,1,0:T(8,128)} fusion(f32[16,128,128]{2,1,0:T(8,128)S(1)} %copy-done, f32[1,16,128,128]{3,2,1,0:T(8,128)} %param.5), kind=kOutput, calls=%fused_computation.2 | convolution fusion | flops 201326592 | bytes 3145728 | tf_op jit(solution)/shard_map/kij,kjl->kil/dot_general | solution.py:298
  14.4 83.6 %shard_map.59.u_in = f32[16,16,128,128]{3,2,1,0:T(8,128)} custom-call(f32[16,128,128]{2,1,0:T(8,128)} %fusion.1.u_ref), custom_call_target="tpu_custom_call" | custom-call | tf_op jit(solution)/shard_map/pallas_call | solution.py:71
  98.0 0.0 all-gather.2.cloned.1.call-done.sig_ref
  98.1 96.8 %shard_map.60 = (f32[16,16,128,128]{3,2,1,0:T(8,128)}, f32[16,3,128,128]{3,2,1,0:T(8,128)}, f32[1,128,128]{2,1,0:T(8,128)}) custom-call(s32[16,16]{1,0:T(8,128)} %struct_ref.1, s32[16,3]{1,0:T(8,128)} %copy.9.hit_ref, s32[16,3]{1,0:T(8,128)} %copy.10.slot_ref, ...), custom_call_target="tpu_custom_call", output_to_operand_aliasing={{0}: (4, {})} | custom-call | flops 9663676416 | bytes 26214400 | tf_op jit(solution)/shard_map/pallas_call | solution.py:256
  194.8 1.7 fusion
  196.6 3.9 %copy.13 = f32[16,3,128,128]{3,2,1,0:T(8,128)} copy(f32[16,3,128,128]{3,2,1,0:T(8,128)} %get-tuple-element.10) | data formatting | bytes 6291456
  (2 shorter events, 0.0 us)
Async XLA Ops:
  7.2 4.5 %copy-start = (f32[16,128,128]{2,1,0:T(8,128)S(1)}, f32[16,128,128]{2,1,0:T(8,128)}, u32[]{:S(2)}) copy-start(f32[16,128,128]{2,1,0:T(8,128)} %param.6) | copy-start | bytes 3145732
  7.2 90.9 %all-gather.2.cloned.1.call-start = ((), (), s32[]{:S(2)}) async-start(), calls=%async_computation | async-start | bytes 10027008 | tf_op jit(solution)/shard_map/all_gather | solution.py:297
Sparse Core Ops, SparseCore 0:
  10.4 84.5 all-gather.1

commit v10 on v9

--- a/solution.py
+++ b/solution.py
@@ -82,11 +82,11 @@
     )(u_local)
 
 
-def fused_kernel(first, parts, struct_ref, hit_ref, slot_ref, sig_ref, u_in, u_out, zoff_ref, sum_ref,
+def fused_kernel(first, parts, struct_ref, hit_ref, slot_ref, sig_ref, u_in, zoff_ref, sum_ref,
                  u_vmem, y_acc, part_ref, gather_buf, load_sem, send_sem, recv_sem, out_sem, in_sem):
-    n = u_out.shape[0]
+    n = u_in.shape[0]
     half = n // 2
-    nodes = u_out.shape[1]
+    nodes = u_in.shape[1]
     chunk = nodes // parts
     rows = sig_ref.shape[0]
     width = sig_ref.shape[-1]
@@ -101,14 +101,15 @@
             slot = lax.rem(me + (step - 1), n)
             peer = lax.rem(me + n - 1, n)
         piece = pl.ds(part * chunk, chunk)
+        source = u_in if step == first + 1 else u_vmem
         return pltpu.make_async_remote_copy(
-            src_ref=u_out.at[slot, piece], dst_ref=u_out.at[slot, piece],
+            src_ref=source.at[slot, piece], dst_ref=u_vmem.at[slot, piece],
             send_sem=send_sem.at[direction, step - 1 - first, part],
             recv_sem=recv_sem.at[direction, step - 1 - first, part],
             device_id=(peer, col), device_id_type=pl.DeviceIdType.MESH)
 
     def load(slot):
-        return pltpu.make_async_copy(u_out.at[slot], u_vmem.at[slot], load_sem.at[slot])
+        return pltpu.make_async_copy(u_in.at[slot], u_vmem.at[slot], load_sem.at[slot])
 
     def wrap(offset):
         return lax.rem(me + offset + 2 * n, n)
@@ -156,21 +157,12 @@
                 link(step, direction, part).wait_recv()
         if step < half:
             send_step(step + 1)
-            load(wrap(-step)).start()
-            load(wrap(step)).start()
-        else:
-            load(wrap(half)).start()
 
     def arrived(step):
         if step < half:
-            one, two = wrap(-step), wrap(step)
-            load(one).wait()
-            load(two).wait()
-            add_pair(one, two)
+            add_pair(wrap(-step), wrap(step))
         else:
-            last = wrap(half)
-            load(last).wait()
-            add_single(last)
+            add_single(wrap(half))
 
     processed = first
     load(me).wait()
@@ -195,7 +187,6 @@
         processed += 1
         ring_event(processed)
     last = wrap(half)
-    load(last).wait()
 
     for copy in started:
         copy.wait_send()
@@ -256,7 +247,6 @@
     return pl.pallas_call(
         functools.partial(fused_kernel, first, parts),
         out_shape=[
-            jax.ShapeDtypeStruct(u_all.shape, jnp.float32),
             jax.ShapeDtypeStruct((nodes, rows, width, width), jnp.float32),
             jax.ShapeDtypeStruct((1, width, width), jnp.float32),
         ],
@@ -268,7 +258,6 @@
             pl.BlockSpec(memory_space=pl.ANY),
         ],
         out_specs=[
-            pl.BlockSpec(memory_space=pl.ANY),
             pl.BlockSpec(memory_space=pltpu.VMEM),
             pl.BlockSpec(memory_space=pltpu.VMEM),
         ],
@@ -283,7 +272,6 @@
             pltpu.SemaphoreType.DMA((slots,)),
             pltpu.SemaphoreType.DMA((slots,)),
         ],
-        input_output_aliases={4: 0},
         compiler_params=pltpu.CompilerParams(collective_id=1, has_side_effects=True,
                                              vmem_limit_bytes=60 * 1024 * 1024),
         cost_estimate=pl.CostEstimate(flops=flops, transcendentals=0,
@@ -302,7 +290,7 @@
     match = struct[:, :, None] == wanted[None, None, :]
     hit = jnp.any(match, axis=1).astype(jnp.int32)
     slot = jnp.argmax(match, axis=1).astype(jnp.int32)
-    unused_u, z_off, summed = fused_call(struct, hit, slot, sigma_rows, u_head, first, parts)
+    z_off, summed = fused_call(struct, hit, slot, sigma_rows, u_head, first, parts)
     inverse_share = lax.dynamic_slice_in_dim(diag_inv, row_index, 1, 0)
     inverse_part = jnp.einsum("kij,kil->kjl", inverse_share, inverse_share, precision=high)
     return (z_off, inverse_part + summed)

time: 208 us -> 205 us (0.986)
    pallas_call x1, Pallas kernels: 96.8 us -> 94.5 us  [fused_call(): pl.pallas_call(functools.partial(fused_kernel, first, parts), out_shape=[...]
  transfers between devices with their start and end apart: 1 -> 1, of which waited for: 0 -> 0; matrix products, arithmetic and copies ran while one was open for 3% -> 3% of each run, Pallas kernels for 40% -> 41%
where the time goes in v10:
time: 205 us
  Pallas kernels  178 us (87%)
  between operations  14.1 us (7%)
  local copies, waits for them, and re-layouts  5.27 us (3%)
  matrix products  4.52 us (2%)
  other arithmetic  2.36 us (1%)
    pallas_call x1, Pallas kernels, fused_call(): pl.pallas_call(functools.partial(fused_kernel, first, parts), out_shape=[...  94.5 us
    pallas_call x1, Pallas kernels, ring_gather(): pl.pallas_call(functools.partial(ring_kernel, steps, parts), out_shape=ja...  83.6 us
  transfers between devices with their start and end apart: 1, of which 0 were waited for; matrix products, arithmetic and copies ran while one was open for 3% of the time, Pallas kernels for 41%

profile of v10, /device:TPU:1, one launch (start us, length us, event | category | flops | bytes accessed | tf_op | source)
XLA Modules:
  0.0 205.1 jit_solution(11440190203977363430)
XLA Ops:
  7.2 0.0 copy-start
  7.2 0.0 all-gather.2.cloned.1.call-start
  7.2 0.7 all-gather.2.cloned.1.call-update
  7.9 0.9 compare_reduce_fusion.1
  8.9 1.4 compare_reduce_fusion
  10.3 0.7 copy.9.slot_ref
  11.0 0.7 copy.8.hit_ref
  11.6 0.0 copy-done
  11.6 2.8 %fusion.1.u_ref = f32[16,128,128]{2,1,0:T(8,128)} fusion(f32[16,128,128]{2,1,0:T(8,128)S(1)} %copy-done, f32[1,16,128,128]{3,2,1,0:T(8,128)} %param.5), kind=kOutput, calls=%fused_computation.2 | convolution fusion | flops 201326592 | bytes 3145728 | tf_op jit(solution)/shard_map/kij,kjl->kil/dot_general | solution.py:286
  14.4 83.6 %shard_map.59.u_in = f32[16,16,128,128]{3,2,1,0:T(8,128)} custom-call(f32[16,128,128]{2,1,0:T(8,128)} %fusion.1.u_ref), custom_call_target="tpu_custom_call" | custom-call | tf_op jit(solution)/shard_map/pallas_call | solution.py:71
  98.0 0.0 all-gather.2.cloned.1.call-done.sig_ref
  98.1 94.5 %shard_map.60 = (f32[16,3,128,128]{3,2,1,0:T(8,128)}, f32[1,128,128]{2,1,0:T(8,128)}) custom-call(s32[16,16]{1,0:T(8,128)} %struct_ref.1, s32[16,3]{1,0:T(8,128)} %copy.8.hit_ref, s32[16,3]{1,0:T(8,128)} %copy.9.slot_ref, f32[3,48,128,128]{3,2,1,0:T(8,128)} %all-gather.2.cloned.1.call-done.sig_ref, f32[16,16,128,128]{3,2,1,0:T(8,128)} %shard_map.59.u_in), custom_call_target="tpu_custom_call" | custom-call | flops 9663676416 | bytes 26214400 | tf_op jit(solution)/shard_map/pallas_call | solution.py:247
  192.6 1.7 fusion
  194.3 3.9 %copy.11 = f32[16,3,128,128]{3,2,1,0:T(8,128)} copy(f32[16,3,128,128]{3,2,1,0:T(8,128)} %get-tuple-element.10) | data formatting | bytes 6291456
  (2 shorter events, 0.0 us)
Async XLA Ops:
  7.2 4.5 %copy-start = (f32[16,128,128]{2,1,0:T(8,128)S(1)}, f32[16,128,128]{2,1,0:T(8,128)}, u32[]{:S(2)}) copy-start(f32[16,128,128]{2,1,0:T(8,128)} %param.6) | copy-start | bytes 3145732
  7.2 90.9 %all-gather.2.cloned.1.call-start = ((), (), s32[]{:S(2)}) async-start(), calls=%async_computation | async-start | bytes 10027008 | tf_op jit(solution)/shard_map/all_gather | solution.py:285
Sparse Core Ops, SparseCore 0:
  10.4 84.5 all-gather.1

commit v11 on v10

--- a/solution.py
+++ b/solution.py
@@ -82,7 +82,7 @@
     )(u_local)
 
 
-def fused_kernel(first, parts, struct_ref, hit_ref, slot_ref, sig_ref, u_in, zoff_ref, sum_ref,
+def fused_kernel(first, parts, struct_ref, hit_ref, slot_ref, sig_ref, inv_ref, u_in, zoff_ref, sum_ref,
                  u_vmem, y_acc, part_ref, gather_buf, load_sem, send_sem, recv_sem, out_sem, in_sem):
     n = u_in.shape[0]
     half = n // 2
@@ -236,10 +236,13 @@
             share_to(j).wait_send()
             share_from(j).wait_recv()
 
-    sum_ref[0] = jnp.sum(gather_buf[...], axis=0)
-
-
-def fused_call(struct, hit, slot, sigma_rows, u_all, first, parts):
+    inverse = inv_ref[0]
+    inverse_part = jnp.dot(jnp.transpose(inverse), inverse, precision=high,
+                           preferred_element_type=jnp.float32)
+    sum_ref[0] = inverse_part + jnp.sum(gather_buf[...], axis=0)
+
+
+def fused_call(struct, hit, slot, sigma_rows, inverse_share, u_all, first, parts):
     slots, nodes, width, _ = u_all.shape
     rows = sigma_rows.shape[0]
     later = slots // 2 - first
@@ -254,6 +257,7 @@
             pl.BlockSpec(memory_space=pltpu.SMEM),
             pl.BlockSpec(memory_space=pltpu.SMEM),
             pl.BlockSpec(memory_space=pltpu.SMEM),
+            pl.BlockSpec(memory_space=pltpu.VMEM),
             pl.BlockSpec(memory_space=pltpu.VMEM),
             pl.BlockSpec(memory_space=pl.ANY),
         ],
@@ -276,7 +280,7 @@
                                              vmem_limit_bytes=60 * 1024 * 1024),
         cost_estimate=pl.CostEstimate(flops=flops, transcendentals=0,
                                       bytes_accessed=4 * (sigma_rows.size + u_all.size)),
-    )(struct, hit, slot, sigma_rows, u_all)
+    )(struct, hit, slot, sigma_rows, inverse_share, u_all)
 
 
 def body(sigma_anc, factor, diag_inv, struct):
@@ -286,14 +290,14 @@
     u_local = jnp.einsum("kij,kjl->kil", factor[0], diag_inv, precision=high)
     first, parts = 4, 4
     u_head = ring_gather(u_local, lax.axis_size("row"), first, parts)
+    struct, u_head = lax.optimization_barrier((struct, u_head))
     wanted = row_index * row_count + jnp.arange(row_count, dtype=jnp.int32)
     match = struct[:, :, None] == wanted[None, None, :]
     hit = jnp.any(match, axis=1).astype(jnp.int32)
     slot = jnp.argmax(match, axis=1).astype(jnp.int32)
-    z_off, summed = fused_call(struct, hit, slot, sigma_rows, u_head, first, parts)
     inverse_share = lax.dynamic_slice_in_dim(diag_inv, row_index, 1, 0)
-    inverse_part = jnp.einsum("kij,kil->kjl", inverse_share, inverse_share, precision=high)
-    return (z_off, inverse_part + summed)
+    z_off, z_diag = fused_call(struct, hit, slot, sigma_rows, inverse_share, u_head, first, parts)
+    return (z_off, z_diag)
 
 
 def solution(mesh):

time: 205 us -> 205 us (level)
  local copies, waits for them, and re-layouts: 5.27 us -> 7.86 us
    unnamed x3 -> x6, local copies, waits for them, and re-layouts: 3.92 us -> 5.87 us
where the time goes in v11:
time: 205 us; the launch traced here: 204 us
  Pallas kernels  178 us (87%)
  between operations  14.1 us (7%)
  local copies, waits for them, and re-layouts  7.86 us (4%)
  matrix products  2.79 us (1%)
    pallas_call x1, Pallas kernels, fused_call(): pl.pallas_call(functools.partial(fused_kernel, first, parts), out_shape=[...  94.3 us
    pallas_call x1, Pallas kernels, ring_gather(): pl.pallas_call(functools.partial(ring_kernel, steps, parts), out_shape=ja...  83.6 us
    unnamed x6, local copies, waits for them, and re-layouts  5.87 us
  transfers between devices with their start and end apart: 1, of which 0 were waited for; matrix products, arithmetic and copies ran while one was open for 3% of the time, Pallas kernels for 41%

profile of v11, /device:TPU:1, one launch (start us, length us, event | category | flops | bytes accessed | tf_op | source)
XLA Modules:
  0.0 204.3 jit_solution(5343836003990400874)
XLA Ops:
  7.2 0.0 copy-start
  7.2 0.0 all-gather.2.cloned.1.call-start
  7.2 0.7 all-gather.2.cloned.1.call-update
  7.9 0.5 copy-done
  8.4 2.8 %fusion.u_ref = f32[16,128,128]{2,1,0:T(8,128)} fusion(f32[16,128,128]{2,1,0:T(8,128)S(1)} %copy-done, f32[1,16,128,128]{3,2,1,0:T(8,128)} %param.5), kind=kOutput, calls=%fused_computation | convolution fusion | flops 201326592 | bytes 3145728 | tf_op jit(solution)/shard_map/kij,kjl->kil/dot_general | solution.py:290
  11.2 0.0 copy-start.1
  11.2 83.6 %shard_map.59.u_in = f32[16,16,128,128]{3,2,1,0:T(8,128)} custom-call(f32[16,128,128]{2,1,0:T(8,128)} %fusion.u_ref), custom_call_target="tpu_custom_call" | custom-call | tf_op jit(solution)/shard_map/pallas_call | solution.py:71
  94.8 0.0 copy-done.1
  94.8 0.2 compare_reduce_fusion.1
  95.0 0.7 compare_reduce_fusion
  95.8 0.7 copy.9.slot_ref
  96.5 0.7 copy.8.hit_ref
  97.1 0.6 constant_dynamic-slice_fusion.inv_ref
  97.8 0.0 all-gather.2.cloned.1.call-done.sig_ref
  97.8 94.3 %shard_map.60 = (f32[16,3,128,128]{3,2,1,0:T(8,128)}, f32[1,128,128]{2,1,0:T(8,128)}) custom-call(s32[16,16]{1,0:T(8,128)} %struct_ref, s32[16,3]{1,0:T(8,128)} %copy.8.hit_ref, s32[16,3]{1,0:T(8,128)} %copy.9.slot_ref, f32[3,48,128,128]{3,2,1,0:T(8,128)} %all-gather.2.cloned.1.call-done.sig_ref, f32[1,128,128]{2,1,0:T(8,128)} %constant_dynamic-slice_fusion.inv_ref, ...), custom_call_target="tpu_custom_call" | custom-call | flops 9663676416 | bytes 26214400 | tf_op jit(solution)/shard_map/pallas_call | solution.py:250
  192.1 3.9 %copy.12 = f32[16,3,128,128]{3,2,1,0:T(8,128)} copy(f32[16,3,128,128]{3,2,1,0:T(8,128)} %get-tuple-element.10) | data formatting | bytes 6291456
  196.0 1.5 copy.13
  (2 shorter events, 0.0 us)
Async XLA Ops:
  7.2 1.2 copy-start
  7.2 90.6 %all-gather.2.cloned.1.call-start = ((), (), s32[]{:S(2)}) async-start(), calls=%async_computation | async-start | bytes 10027008 | tf_op jit(solution)/shard_map/all_gather | solution.py:289
  11.2 83.6 %copy-start.1 = (s32[16,16]{1,0:T(8,128)S(1)}, s32[16,16]{1,0:T(8,128)}, u32[]{:S(2)}) copy-start(s32[16,16]{1,0:T(8,128)} %struct_ref) | copy-start | bytes 3076
Sparse Core Ops, SparseCore 0:
  10.4 84.5 all-gather.1

commit v12 on v11

--- a/solution.py
+++ b/solution.py
@@ -25,7 +25,7 @@
     return range(parts // 2, parts)
 
 
-def ring_kernel(steps, parts, u_ref, out_ref, copy_sem, send_sem, recv_sem):
+def ring_kernel(steps, parts, rows, struct_ref, u_ref, out_ref, hit_ref, slot_ref, copy_sem, send_sem, recv_sem):
     n = out_ref.shape[0]
     chunk = out_ref.shape[1] // parts
     me = lax.axis_index("row")
@@ -59,6 +59,20 @@
                 copy = link(step, direction, part)
                 copy.start()
                 started.append(copy)
+        if step == 1:
+            base = me * rows
+
+            def member(k, carry):
+                for j in range(rows):
+                    def scan(s, acc):
+                        hit = (struct_ref[k, s] == base + j).astype(jnp.int32)
+                        return acc[0] + hit, acc[1] + hit * s
+                    hits, slot = lax.fori_loop(0, n, scan, (jnp.int32(0), jnp.int32(0)))
+                    hit_ref[k, j] = hits
+                    slot_ref[k, j] = slot
+                return carry
+
+            lax.fori_loop(0, struct_ref.shape[0], member, 0)
     for direction in (0, 1):
         for part in range(parts):
             link(steps, direction, part).wait_recv()
@@ -66,24 +80,33 @@
         copy.wait_send()
 
 
-def ring_gather(u_local, slots, steps, parts):
+def ring_gather(struct, u_local, slots, rows, steps, parts):
     nodes, width, _ = u_local.shape
     return pl.pallas_call(
-        functools.partial(ring_kernel, steps, parts),
-        out_shape=jax.ShapeDtypeStruct((slots, nodes, width, width), jnp.float32),
-        in_specs=[pl.BlockSpec(memory_space=pl.ANY)],
-        out_specs=pl.BlockSpec(memory_space=pl.ANY),
+        functools.partial(ring_kernel, steps, parts, rows),
+        out_shape=[
+            jax.ShapeDtypeStruct((slots, nodes, width, width), jnp.float32),
+            jax.ShapeDtypeStruct((nodes, rows), jnp.int32),
+            jax.ShapeDtypeStruct((nodes, rows), jnp.int32),
+        ],
+        in_specs=[pl.BlockSpec(memory_space=pltpu.SMEM), pl.BlockSpec(memory_space=pl.ANY)],
+        out_specs=[
+            pl.BlockSpec(memory_space=pl.ANY),
+            pl.BlockSpec(memory_space=pltpu.SMEM),
+            pl.BlockSpec(memory_space=pltpu.SMEM),
+        ],
         scratch_shapes=[
             pltpu.SemaphoreType.DMA((1,)),
             pltpu.SemaphoreType.DMA((2, steps, parts)),
             pltpu.SemaphoreType.DMA((2, steps, parts)),
         ],
         compiler_params=pltpu.CompilerParams(collective_id=0, has_side_effects=True),
-    )(u_local)
+    )(struct, u_local)
 
 
 def fused_kernel(first, parts, struct_ref, hit_ref, slot_ref, sig_ref, inv_ref, u_in, zoff_ref, sum_ref,
-                 u_vmem, y_acc, part_ref, gather_buf, load_sem, send_sem, recv_sem, out_sem, in_sem):
+                 u_vmem, y_acc, part_ref, gather_buf, inv_vmem, load_sem, send_sem, recv_sem, out_sem, in_sem,
+                 inv_sem):
     n = u_in.shape[0]
     half = n // 2
     nodes = u_in.shape[1]
@@ -121,6 +144,8 @@
     pl.semaphore_wait(barrier, n - 1)
     for offset in range(-first, first + 1):
         load(wrap(offset)).start()
+    inv_copy = pltpu.make_async_copy(inv_ref.at[me], inv_vmem, inv_sem.at[0])
+    inv_copy.start()
 
     started = []
 
@@ -236,7 +261,8 @@
             share_to(j).wait_send()
             share_from(j).wait_recv()
 
-    inverse = inv_ref[0]
+    inv_copy.wait()
+    inverse = inv_vmem[...]
     inverse_part = jnp.dot(jnp.transpose(inverse), inverse, precision=high,
                            preferred_element_type=jnp.float32)
     sum_ref[0] = inverse_part + jnp.sum(gather_buf[...], axis=0)
@@ -258,7 +284,7 @@
             pl.BlockSpec(memory_space=pltpu.SMEM),
             pl.BlockSpec(memory_space=pltpu.SMEM),
             pl.BlockSpec(memory_space=pltpu.VMEM),
-            pl.BlockSpec(memory_space=pltpu.VMEM),
+            pl.BlockSpec(memory_space=pl.ANY),
             pl.BlockSpec(memory_space=pl.ANY),
         ],
         out_specs=[
@@ -270,11 +296,13 @@
             pltpu.VMEM((nodes, rows * width, width), jnp.float32),
             pltpu.VMEM((nodes, width, width), jnp.float32),
             pltpu.VMEM((slots, width, width), jnp.float32),
+            pltpu.VMEM((width, width), jnp.float32),
             pltpu.SemaphoreType.DMA((slots,)),
             pltpu.SemaphoreType.DMA((2, later, parts)),
             pltpu.SemaphoreType.DMA((2, later, parts)),
             pltpu.SemaphoreType.DMA((slots,)),
             pltpu.SemaphoreType.DMA((slots,)),
+            pltpu.SemaphoreType.DMA((1,)),
         ],
         compiler_params=pltpu.CompilerParams(collective_id=1, has_side_effects=True,
                                              vmem_limit_bytes=60 * 1024 * 1024),
@@ -285,18 +313,11 @@
 
 def body(sigma_anc, factor, diag_inv, struct):
     row_count = sigma_anc.shape[0]
-    row_index = lax.axis_index("row")
     sigma_rows = lax.all_gather(sigma_anc, "col", axis=1, tiled=True)
     u_local = jnp.einsum("kij,kjl->kil", factor[0], diag_inv, precision=high)
     first, parts = 4, 4
-    u_head = ring_gather(u_local, lax.axis_size("row"), first, parts)
-    struct, u_head = lax.optimization_barrier((struct, u_head))
-    wanted = row_index * row_count + jnp.arange(row_count, dtype=jnp.int32)
-    match = struct[:, :, None] == wanted[None, None, :]
-    hit = jnp.any(match, axis=1).astype(jnp.int32)
-    slot = jnp.argmax(match, axis=1).astype(jnp.int32)
-    inverse_share = lax.dynamic_slice_in_dim(diag_inv, row_index, 1, 0)
-    z_off, z_diag = fused_call(struct, hit, slot, sigma_rows, inverse_share, u_head, first, parts)
+    u_head, hit, slot = ring_gather(struct, u_local, lax.axis_size("row"), row_count, first, parts)
+    z_off, z_diag = fused_call(struct, hit, slot, sigma_rows, diag_inv, u_head, first, parts)
     return (z_off, z_diag)
 
 

time: 205 us -> 203 us (level)
    unnamed x6 -> x4, local copies, waits for them, and re-layouts: 5.87 us -> 5.87 us
  transfers between devices with their start and end apart: 1 -> 1, of which waited for: 0 -> 0; matrix products, arithmetic and copies ran while one was open for 3% -> 1% of each run, Pallas kernels for 41% -> 42%
where the time goes in v12:
time: 203 us
  Pallas kernels  180 us (89%)
  between operations  14.1 us (7%)
  local copies, waits for them, and re-layouts  5.87 us (3%)
  matrix products  2.79 us (1%)
    pallas_call x1, Pallas kernels, fused_call(): pl.pallas_call(functools.partial(fused_kernel, first, parts), out_shape=[...  94.5 us
    pallas_call x1, Pallas kernels, ring_gather(): pl.pallas_call(functools.partial(ring_kernel, steps, parts, rows), out_sh...  85.2 us
    unnamed x4, local copies, waits for them, and re-layouts  5.87 us
  transfers between devices with their start and end apart: 1, of which 0 were waited for; matrix products, arithmetic and copies ran while one was open for 1% of the time, Pallas kernels for 42%

profile of v12, /device:TPU:1, one launch (start us, length us, event | category | flops | bytes accessed | tf_op | source)
XLA Modules:
  0.0 203.2 jit_solution(7608692269340809820)
XLA Ops:
  7.2 0.0 copy-start
  7.2 0.0 all-gather.2.cloned.1.call-start
  7.2 0.7 all-gather.2.cloned.1.call-update
  7.9 0.5 copy-done
  8.4 2.8 %fusion.u_ref = f32[16,128,128]{2,1,0:T(8,128)} fusion(f32[16,128,128]{2,1,0:T(8,128)} %inv_ref.1, f32[1,16,128,128]{3,2,1,0:T(8,128)S(1)} %copy-done), kind=kOutput, calls=%fused_computation | convolution fusion | flops 201326592 | bytes 3145728 | tf_op jit(solution)/shard_map/kij,kjl->kil/dot_general | solution.py:317
  11.2 85.2 %shard_map.59 = (f32[16,16,128,128]{3,2,1,0:T(8,128)}, s32[16,3]{1,0:T(8,128)}, s32[16,3]{1,0:T(8,128)}) custom-call(s32[16,16]{1,0:T(8,128)} %struct_ref.3, f32[16,128,128]{2,1,0:T(8,128)} %fusion.u_ref), custom_call_target="tpu_custom_call" | custom-call | tf_op jit(solution)/shard_map/pallas_call | solution.py:85
  96.4 0.0 all-gather.2.cloned.1.call-done.sig_ref
  96.4 94.5 %shard_map.60 = (f32[16,3,128,128]{3,2,1,0:T(8,128)}, f32[1,128,128]{2,1,0:T(8,128)}) custom-call(s32[16,16]{1,0:T(8,128)} %struct_ref.3, s32[16,3]{1,0:T(8,128)} %get-tuple-element.5.hit_ref, s32[16,3]{1,0:T(8,128)} %get-tuple-element.6.slot_ref, f32[3,48,128,128]{3,2,1,0:T(8,128)} %all-gather.2.cloned.1.call-done.sig_ref, f32[16,128,128]{2,1,0:T(8,128)} %inv_ref.1, ...), custom_call_target="tpu_custom_call" | custom-call | flops 9663676416 | bytes 26214400 | tf_op jit(solution)/shard_map/pallas_call | solution.py:276
  190.9 3.9 %copy.8 = f32[16,3,128,128]{3,2,1,0:T(8,128)} copy(f32[16,3,128,128]{3,2,1,0:T(8,128)} %get-tuple-element.10) | data formatting | bytes 6291456
  194.8 1.5 copy.9
Async XLA Ops:
  7.2 1.2 copy-start
  7.2 89.2 %all-gather.2.cloned.1.call-start = ((), (), s32[]{:S(2)}) async-start(), calls=%async_computation | async-start | bytes 10027008 | tf_op jit(solution)/shard_map/all_gather | solution.py:316
Sparse Core Ops, SparseCore 0:
  10.4 84.5 all-gather.1

commit v13 on v12

--- a/solution.py
+++ b/solution.py
@@ -315,7 +315,7 @@
     row_count = sigma_anc.shape[0]
     sigma_rows = lax.all_gather(sigma_anc, "col", axis=1, tiled=True)
     u_local = jnp.einsum("kij,kjl->kil", factor[0], diag_inv, precision=high)
-    first, parts = 4, 4
+    first, parts = 4, 8
     u_head, hit, slot = ring_gather(struct, u_local, lax.axis_size("row"), row_count, first, parts)
     z_off, z_diag = fused_call(struct, hit, slot, sigma_rows, diag_inv, u_head, first, parts)
     return (z_off, z_diag)

time: 203 us -> 205 us (level)
  no operation moved by 1% of the time
where the time goes in v13:
time: 205 us; the launch traced here: 204 us
  Pallas kernels  181 us (88%)
  between operations  14.1 us (7%)
  local copies, waits for them, and re-layouts  5.87 us (3%)
  matrix products  2.79 us (1%)
    pallas_call x1, Pallas kernels, fused_call(): pl.pallas_call(functools.partial(fused_kernel, first, parts), out_shape=[...  95.2 us
    pallas_call x1, Pallas kernels, ring_gather(): pl.pallas_call(functools.partial(ring_kernel, steps, parts, rows), out_sh...  85.8 us
    unnamed x4, local copies, waits for them, and re-layouts  5.87 us
  transfers between devices with their start and end apart: 1, of which 0 were waited for; matrix products, arithmetic and copies ran while one was open for 1% of the time, Pallas kernels for 42%

profile of v13, /device:TPU:1, one launch (start us, length us, event | category | flops | bytes accessed | tf_op | source)
XLA Modules:
  0.0 204.4 jit_solution(14304728264413881936)
XLA Ops:
  7.2 0.0 copy-start
  7.2 0.0 all-gather.2.cloned.1.call-start
  7.2 0.7 all-gather.2.cloned.1.call-update
  7.9 0.5 copy-done
  8.4 2.8 %fusion.u_ref = f32[16,128,128]{2,1,0:T(8,128)} fusion(f32[16,128,128]{2,1,0:T(8,128)} %inv_ref.1, f32[1,16,128,128]{3,2,1,0:T(8,128)S(1)} %copy-done), kind=kOutput, calls=%fused_computation | convolution fusion | flops 201326592 | bytes 3145728 | tf_op jit(solution)/shard_map/kij,kjl->kil/dot_general | solution.py:317
  11.2 85.8 %shard_map.59 = (f32[16,16,128,128]{3,2,1,0:T(8,128)}, s32[16,3]{1,0:T(8,128)}, s32[16,3]{1,0:T(8,128)}) custom-call(s32[16,16]{1,0:T(8,128)} %struct_ref.3, f32[16,128,128]{2,1,0:T(8,128)} %fusion.u_ref), custom_call_target="tpu_custom_call" | custom-call | tf_op jit(solution)/shard_map/pallas_call | solution.py:85
  97.0 0.0 all-gather.2.cloned.1.call-done.sig_ref
  97.0 95.2 %shard_map.60 = (f32[16,3,128,128]{3,2,1,0:T(8,128)}, f32[1,128,128]{2,1,0:T(8,128)}) custom-call(s32[16,16]{1,0:T(8,128)} %struct_ref.3, s32[16,3]{1,0:T(8,128)} %get-tuple-element.5.hit_ref, s32[16,3]{1,0:T(8,128)} %get-tuple-element.6.slot_ref, f32[3,48,128,128]{3,2,1,0:T(8,128)} %all-gather.2.cloned.1.call-done.sig_ref, f32[16,128,128]{2,1,0:T(8,128)} %inv_ref.1, ...), custom_call_target="tpu_custom_call" | custom-call | flops 9663676416 | bytes 26214400 | tf_op jit(solution)/shard_map/pallas_call | solution.py:276
  192.2 3.9 %copy.8 = f32[16,3,128,128]{3,2,1,0:T(8,128)} copy(f32[16,3,128,128]{3,2,1,0:T(8,128)} %get-tuple-element.10) | data formatting | bytes 6291456
  196.1 1.5 copy.9
Async XLA Ops:
  7.2 1.2 copy-start
  7.2 89.8 %all-gather.2.cloned.1.call-start = ((), (), s32[]{:S(2)}) async-start(), calls=%async_computation | async-start | bytes 10027008 | tf_op jit(solution)/shard_map/all_gather | solution.py:316
Sparse Core Ops, SparseCore 0:
  10.4 84.5 all-gather.1

commit v14 on v12

--- a/solution.py
+++ b/solution.py
@@ -59,17 +59,17 @@
                 copy = link(step, direction, part)
                 copy.start()
                 started.append(copy)
-        if step == 1:
-            base = me * rows
+        if step <= rows:
+            j = step - 1
+            base = me * rows + j
 
             def member(k, carry):
-                for j in range(rows):
-                    def scan(s, acc):
-                        hit = (struct_ref[k, s] == base + j).astype(jnp.int32)
-                        return acc[0] + hit, acc[1] + hit * s
-                    hits, slot = lax.fori_loop(0, n, scan, (jnp.int32(0), jnp.int32(0)))
-                    hit_ref[k, j] = hits
-                    slot_ref[k, j] = slot
+                def scan(s, acc):
+                    hit = (struct_ref[k, s] == base).astype(jnp.int32)
+                    return acc[0] + hit, acc[1] + hit * s
+                hits, slot = lax.fori_loop(0, n, scan, (jnp.int32(0), jnp.int32(0)))
+                hit_ref[k, j] = hits
+                slot_ref[k, j] = slot
                 return carry
 
             lax.fori_loop(0, struct_ref.shape[0], member, 0)

time: 203 us -> 203 us (level)
  no operation moved by 1% of the time
where the time goes in v14:
time: 203 us
  Pallas kernels  180 us (89%)
  between operations  14.1 us (7%)
  local copies, waits for them, and re-layouts  5.87 us (3%)
  matrix products  2.79 us (1%)
    pallas_call x1, Pallas kernels, fused_call(): pl.pallas_call(functools.partial(fused_kernel, first, parts), out_shape=[...  94.5 us
    pallas_call x1, Pallas kernels, ring_gather(): pl.pallas_call(functools.partial(ring_kernel, steps, parts, rows), out_sh...  85.2 us
    unnamed x4, local copies, waits for them, and re-layouts  5.87 us
  transfers between devices with their start and end apart: 1, of which 0 were waited for; matrix products, arithmetic and copies ran while one was open for 1% of the time, Pallas kernels for 42%

profile of v14, /device:TPU:1, one launch (start us, length us, event | category | flops | bytes accessed | tf_op | source)
XLA Modules:
  0.0 203.2 jit_solution(10260931197358405169)
XLA Ops:
  7.2 0.0 copy-start
  7.2 0.0 all-gather.2.cloned.1.call-start
  7.2 0.7 all-gather.2.cloned.1.call-update
  7.9 0.5 copy-done
  8.4 2.8 %fusion.u_ref = f32[16,128,128]{2,1,0:T(8,128)} fusion(f32[16,128,128]{2,1,0:T(8,128)} %inv_ref.1, f32[1,16,128,128]{3,2,1,0:T(8,128)S(1)} %copy-done), kind=kOutput, calls=%fused_computation | convolution fusion | flops 201326592 | bytes 3145728 | tf_op jit(solution)/shard_map/kij,kjl->kil/dot_general | solution.py:317
  11.2 85.2 %shard_map.59 = (f32[16,16,128,128]{3,2,1,0:T(8,128)}, s32[16,3]{1,0:T(8,128)}, s32[16,3]{1,0:T(8,128)}) custom-call(s32[16,16]{1,0:T(8,128)} %struct_ref.3, f32[16,128,128]{2,1,0:T(8,128)} %fusion.u_ref), custom_call_target="tpu_custom_call" | custom-call | tf_op jit(solution)/shard_map/pallas_call | solution.py:85
  96.4 0.0 all-gather.2.cloned.1.call-done.sig_ref
  96.4 94.5 %shard_map.60 = (f32[16,3,128,128]{3,2,1,0:T(8,128)}, f32[1,128,128]{2,1,0:T(8,128)}) custom-call(s32[16,16]{1,0:T(8,128)} %struct_ref.3, s32[16,3]{1,0:T(8,128)} %get-tuple-element.5.hit_ref, s32[16,3]{1,0:T(8,128)} %get-tuple-element.6.slot_ref, f32[3,48,128,128]{3,2,1,0:T(8,128)} %all-gather.2.cloned.1.call-done.sig_ref, f32[16,128,128]{2,1,0:T(8,128)} %inv_ref.1, ...), custom_call_target="tpu_custom_call" | custom-call | flops 9663676416 | bytes 26214400 | tf_op jit(solution)/shard_map/pallas_call | solution.py:276
  190.9 3.9 %copy.8 = f32[16,3,128,128]{3,2,1,0:T(8,128)} copy(f32[16,3,128,128]{3,2,1,0:T(8,128)} %get-tuple-element.10) | data formatting | bytes 6291456
  194.8 1.5 copy.9
Async XLA Ops:
  7.2 1.2 copy-start
  7.2 89.2 %all-gather.2.cloned.1.call-start = ((), (), s32[]{:S(2)}) async-start(), calls=%async_computation | async-start | bytes 10027008 | tf_op jit(solution)/shard_map/all_gather | solution.py:316
Sparse Core Ops, SparseCore 0:
  10.4 84.5 all-gather.1

commit v15 on v14

--- a/solution.py
+++ b/solution.py
@@ -25,7 +25,8 @@
     return range(parts // 2, parts)
 
 
-def ring_kernel(steps, parts, rows, struct_ref, u_ref, out_ref, hit_ref, slot_ref, copy_sem, send_sem, recv_sem):
+def ring_kernel(steps, parts, rows, struct_ref, factor_ref, inv_ref, out_ref, hit_ref, slot_ref, u_scr,
+                copy_sem, send_sem, recv_sem):
     n = out_ref.shape[0]
     chunk = out_ref.shape[1] // parts
     me = lax.axis_index("row")
@@ -45,9 +46,14 @@
             recv_sem=recv_sem.at[direction, step - 1, part],
             device_id=(peer, col), device_id_type=pl.DeviceIdType.MESH)
 
-    own = pltpu.make_async_copy(u_ref, out_ref.at[me], copy_sem.at[0])
+    def make_u(k, carry):
+        u_scr[k] = jnp.dot(factor_ref[k], inv_ref[k], precision=high, preferred_element_type=jnp.float32)
+        return carry
+
+    lax.fori_loop(0, u_scr.shape[0], make_u, 0)
+    greet_neighbours(me, col, n)
+    own = pltpu.make_async_copy(u_scr, out_ref.at[me], copy_sem.at[0])
     own.start()
-    greet_neighbours(me, col, n)
     own.wait()
 
     started = []
@@ -80,8 +86,8 @@
         copy.wait_send()
 
 
-def ring_gather(struct, u_local, slots, rows, steps, parts):
-    nodes, width, _ = u_local.shape
+def ring_gather(struct, factor_own, diag_inv, slots, rows, steps, parts):
+    nodes, width, _ = diag_inv.shape
     return pl.pallas_call(
         functools.partial(ring_kernel, steps, parts, rows),
         out_shape=[
@@ -89,19 +95,21 @@
             jax.ShapeDtypeStruct((nodes, rows), jnp.int32),
             jax.ShapeDtypeStruct((nodes, rows), jnp.int32),
         ],
-        in_specs=[pl.BlockSpec(memory_space=pltpu.SMEM), pl.BlockSpec(memory_space=pl.ANY)],
+        in_specs=[pl.BlockSpec(memory_space=pltpu.SMEM), pl.BlockSpec(memory_space=pltpu.VMEM),
+                  pl.BlockSpec(memory_space=pltpu.VMEM)],
         out_specs=[
             pl.BlockSpec(memory_space=pl.ANY),
             pl.BlockSpec(memory_space=pltpu.SMEM),
             pl.BlockSpec(memory_space=pltpu.SMEM),
         ],
         scratch_shapes=[
+            pltpu.VMEM((nodes, width, width), jnp.float32),
             pltpu.SemaphoreType.DMA((1,)),
             pltpu.SemaphoreType.DMA((2, steps, parts)),
             pltpu.SemaphoreType.DMA((2, steps, parts)),
         ],
         compiler_params=pltpu.CompilerParams(collective_id=0, has_side_effects=True),
-    )(struct, u_local)
+    )(struct, factor_own, diag_inv)
 
 
 def fused_kernel(first, parts, struct_ref, hit_ref, slot_ref, sig_ref, inv_ref, u_in, zoff_ref, sum_ref,
@@ -314,9 +322,8 @@
 def body(sigma_anc, factor, diag_inv, struct):
     row_count = sigma_anc.shape[0]
     sigma_rows = lax.all_gather(sigma_anc, "col", axis=1, tiled=True)
-    u_local = jnp.einsum("kij,kjl->kil", factor[0], diag_inv, precision=high)
     first, parts = 4, 4
-    u_head, hit, slot = ring_gather(struct, u_local, lax.axis_size("row"), row_count, first, parts)
+    u_head, hit, slot = ring_gather(struct, factor[0], diag_inv, lax.axis_size("row"), row_count, first, parts)
     z_off, z_diag = fused_call(struct, hit, slot, sigma_rows, diag_inv, u_head, first, parts)
     return (z_off, z_diag)
 

time: 203 us -> 200 us (0.985)
  Pallas kernels: 180 us -> 153 us
  waiting for transfers between devices: 0.7 us -> 27.6 us
  matrix products: 2.79 us -> 0 us
    all_gather x1, waiting for transfers between devices: 0.02 us -> 27 us  [body(): sigma_rows = lax.all_gather(sigma_anc, 'col', axis=1, tiled=True)]
    pallas_call x1, Pallas kernels: 85.2 us -> 60.2 us  [ring_gather(): pl.pallas_call(functools.partial(ring_kernel, steps, parts, rows), out_sh...]
    dot_general x1 -> x0, matrix products: 2.79 us -> none  [body(): u_local = jnp.einsum('kij,kjl->kil', factor[0], diag_inv, precision=high)]
    pallas_call x1, Pallas kernels: 94.5 us -> 92.4 us  [fused_call(): pl.pallas_call(functools.partial(fused_kernel, first, parts), out_shape=[...]
    unnamed x4 -> x2, local copies, waits for them, and re-layouts: 5.87 us -> 5.38 us
  transfers between devices with their start and end apart: 1 -> 1, of which waited for: 0 -> 1; matrix products, arithmetic and copies ran while one was open for 1% -> 0% of each run, Pallas kernels for 42% -> 30%
where the time goes in v15:
time: 200 us
  Pallas kernels  153 us (76%)
  waiting for transfers between devices  27.6 us (14%)
  between operations  14 us (7%)
  local copies, waits for them, and re-layouts  5.38 us (3%)
    pallas_call x1, Pallas kernels, fused_call(): pl.pallas_call(functools.partial(fused_kernel, first, parts), out_shape=[...  92.4 us
    pallas_call x1, Pallas kernels, ring_gather(): pl.pallas_call(functools.partial(ring_kernel, steps, parts, rows), out_sh...  60.2 us
    all_gather x1, waiting for transfers between devices, body(): sigma_rows = lax.all_gather(sigma_anc, 'col', axis=1, tiled=True)  27 us
    unnamed x2, local copies, waits for them, and re-layouts  5.38 us
  transfers between devices with their start and end apart: 1, of which 1 were waited for; matrix products, arithmetic and copies ran while one was open for 0% of the time, Pallas kernels for 30%

profile of v15, /device:TPU:1, one launch (start us, length us, event | category | flops | bytes accessed | tf_op | source)
XLA Modules:
  0.0 199.7 jit_solution(18094178653642319226)
XLA Ops:
  7.2 0.0 all-gather.2.cloned.1.call-start
  7.2 0.7 all-gather.2.cloned.1.call-update
  7.9 60.2 %shard_map.59 = (f32[16,16,128,128]{3,2,1,0:T(8,128)}, s32[16,3]{1,0:T(8,128)}, s32[16,3]{1,0:T(8,128)}) custom-call(s32[16,16]{1,0:T(8,128)} %struct_ref.3, f32[16,128,128]{2,1,0:T(8,128)} %bitcast.1, f32[16,128,128]{2,1,0:T(8,128)} %inv_ref.3), custom_call_target="tpu_custom_call" | custom-call | tf_op jit(solution)/shard_map/pallas_call | solution.py:91
  68.1 27.0 %all-gather.2.cloned.1.call-done.sig_ref = f32[3,48,128,128]{3,2,1,0:T(8,128)} async-done(((f32[3,3,128,128]{3,2,1,0:T(8,128)}), f32[3,48,128,128]{3,2,1,0:T(8,128)}) %all-gather.2.cloned.1.call-update) | async-done | bytes 9437200 | tf_op jit(solution)/shard_map/all_gather | solution.py:324
  95.0 92.4 %shard_map.60 = (f32[16,3,128,128]{3,2,1,0:T(8,128)}, f32[1,128,128]{2,1,0:T(8,128)}) custom-call(s32[16,16]{1,0:T(8,128)} %struct_ref.3, s32[16,3]{1,0:T(8,128)} %get-tuple-element.5.hit_ref, s32[16,3]{1,0:T(8,128)} %get-tuple-element.6.slot_ref, f32[3,48,128,128]{3,2,1,0:T(8,128)} %all-gather.2.cloned.1.call-done.sig_ref, f32[16,128,128]{2,1,0:T(8,128)} %inv_ref.3, ...), custom_call_target="tpu_custom_call" | custom-call | flops 9663676416 | bytes 26214400 | tf_op jit(solution)/shard_map/pallas_call | solution.py:284
  187.4 3.9 %copy.8 = f32[16,3,128,128]{3,2,1,0:T(8,128)} copy(f32[16,3,128,128]{3,2,1,0:T(8,128)} %get-tuple-element.10) | data formatting | bytes 6291456
  191.3 1.5 copy.9
Async XLA Ops:
  7.2 87.9 %all-gather.2.cloned.1.call-start = ((), (), s32[]{:S(2)}) async-start(), calls=%async_computation | async-start | bytes 10027008 | tf_op jit(solution)/shard_map/all_gather | solution.py:324
Sparse Core Ops, SparseCore 0:
  10.4 84.5 all-gather.1

commit v16 on v15

--- a/solution.py
+++ b/solution.py
@@ -322,7 +322,7 @@
 def body(sigma_anc, factor, diag_inv, struct):
     row_count = sigma_anc.shape[0]
     sigma_rows = lax.all_gather(sigma_anc, "col", axis=1, tiled=True)
-    first, parts = 4, 4
+    first, parts = 5, 4
     u_head, hit, slot = ring_gather(struct, factor[0], diag_inv, lax.axis_size("row"), row_count, first, parts)
     z_off, z_diag = fused_call(struct, hit, slot, sigma_rows, diag_inv, u_head, first, parts)
     return (z_off, z_diag)

time: 200 us -> 195 us (0.975)
  waiting for transfers between devices: 27.6 us -> 16.2 us
  Pallas kernels: 153 us -> 160 us
    all_gather x1, waiting for transfers between devices: 27 us -> 15.6 us  [body(): sigma_rows = lax.all_gather(sigma_anc, 'col', axis=1, tiled=True)]
    pallas_call x1, Pallas kernels: 60.2 us -> 71.6 us  [ring_gather(): pl.pallas_call(functools.partial(ring_kernel, steps, parts, rows), out_sh...]
    pallas_call x1, Pallas kernels: 92.4 us -> 87.9 us  [fused_call(): pl.pallas_call(functools.partial(fused_kernel, first, parts), out_shape=[...]
  transfers between devices with their start and end apart: 1 -> 1, of which waited for: 1 -> 1; matrix products, arithmetic and copies ran while one was open for 0% -> 0% of each run, Pallas kernels for 30% -> 37%
where the time goes in v16:
time: 195 us
  Pallas kernels  160 us (82%)
  waiting for transfers between devices  16.2 us (8%)
  between operations  14 us (7%)
  local copies, waits for them, and re-layouts  5.38 us (3%)
    pallas_call x1, Pallas kernels, fused_call(): pl.pallas_call(functools.partial(fused_kernel, first, parts), out_shape=[...  87.9 us
    pallas_call x1, Pallas kernels, ring_gather(): pl.pallas_call(functools.partial(ring_kernel, steps, parts, rows), out_sh...  71.6 us
    all_gather x1, waiting for transfers between devices, body(): sigma_rows = lax.all_gather(sigma_anc, 'col', axis=1, tiled=True)  15.6 us
    unnamed x2, local copies, waits for them, and re-layouts  5.38 us
  transfers between devices with their start and end apart: 1, of which 1 were waited for; matrix products, arithmetic and copies ran while one was open for 0% of the time, Pallas kernels for 37%

profile of v16, /device:TPU:1, one launch (start us, length us, event | category | flops | bytes accessed | tf_op | source)
XLA Modules:
  0.0 195.2 jit_solution(8628369144593279466)
XLA Ops:
  7.2 0.0 all-gather.2.cloned.1.call-start
  7.2 0.7 all-gather.2.cloned.1.call-update
  7.9 71.6 %shard_map.59 = (f32[16,16,128,128]{3,2,1,0:T(8,128)}, s32[16,3]{1,0:T(8,128)}, s32[16,3]{1,0:T(8,128)}) custom-call(s32[16,16]{1,0:T(8,128)} %struct_ref.3, f32[16,128,128]{2,1,0:T(8,128)} %bitcast.1, f32[16,128,128]{2,1,0:T(8,128)} %inv_ref.3), custom_call_target="tpu_custom_call" | custom-call | tf_op jit(solution)/shard_map/pallas_call | solution.py:91
  79.5 15.6 %all-gather.2.cloned.1.call-done.sig_ref = f32[3,48,128,128]{3,2,1,0:T(8,128)} async-done(((f32[3,3,128,128]{3,2,1,0:T(8,128)}), f32[3,48,128,128]{3,2,1,0:T(8,128)}) %all-gather.2.cloned.1.call-update) | async-done | bytes 9437200 | tf_op jit(solution)/shard_map/all_gather | solution.py:324
  95.0 87.9 %shard_map.60 = (f32[16,3,128,128]{3,2,1,0:T(8,128)}, f32[1,128,128]{2,1,0:T(8,128)}) custom-call(s32[16,16]{1,0:T(8,128)} %struct_ref.3, s32[16,3]{1,0:T(8,128)} %get-tuple-element.5.hit_ref, s32[16,3]{1,0:T(8,128)} %get-tuple-element.6.slot_ref, f32[3,48,128,128]{3,2,1,0:T(8,128)} %all-gather.2.cloned.1.call-done.sig_ref, f32[16,128,128]{2,1,0:T(8,128)} %inv_ref.3, ...), custom_call_target="tpu_custom_call" | custom-call | flops 9663676416 | bytes 26214400 | tf_op jit(solution)/shard_map/pallas_call | solution.py:284
  183.0 3.9 %copy.8 = f32[16,3,128,128]{3,2,1,0:T(8,128)} copy(f32[16,3,128,128]{3,2,1,0:T(8,128)} %get-tuple-element.10) | data formatting | bytes 6291456
  186.9 1.5 copy.9
Async XLA Ops:
  7.2 87.9 %all-gather.2.cloned.1.call-start = ((), (), s32[]{:S(2)}) async-start(), calls=%async_computation | async-start | bytes 10027008 | tf_op jit(solution)/shard_map/all_gather | solution.py:324
Sparse Core Ops, SparseCore 0:
  10.4 84.5 all-gather.1

commit v17 on v16

--- a/solution.py
+++ b/solution.py
@@ -322,7 +322,7 @@
 def body(sigma_anc, factor, diag_inv, struct):
     row_count = sigma_anc.shape[0]
     sigma_rows = lax.all_gather(sigma_anc, "col", axis=1, tiled=True)
-    first, parts = 5, 4
+    first, parts = 6, 4
     u_head, hit, slot = ring_gather(struct, factor[0], diag_inv, lax.axis_size("row"), row_count, first, parts)
     z_off, z_diag = fused_call(struct, hit, slot, sigma_rows, diag_inv, u_head, first, parts)
     return (z_off, z_diag)

time: 195 us -> 193 us (0.990)
  waiting for transfers between devices: 16.2 us -> 4.86 us
  Pallas kernels: 160 us -> 168 us
    all_gather x1, waiting for transfers between devices: 15.6 us -> 4.18 us  [body(): sigma_rows = lax.all_gather(sigma_anc, 'col', axis=1, tiled=True)]
    pallas_call x1, Pallas kernels: 71.6 us -> 83 us  [ring_gather(): pl.pallas_call(functools.partial(ring_kernel, steps, parts, rows), out_sh...]
    pallas_call x1, Pallas kernels: 87.9 us -> 85.2 us  [fused_call(): pl.pallas_call(functools.partial(fused_kernel, first, parts), out_shape=[...]
  transfers between devices with their start and end apart: 1 -> 1, of which waited for: 1 -> 1; matrix products, arithmetic and copies ran while one was open for 0% -> 0% of each run, Pallas kernels for 37% -> 43%
where the time goes in v17:
time: 193 us
  Pallas kernels  168 us (87%)
  between operations  14 us (7%)
  local copies, waits for them, and re-layouts  5.38 us (3%)
  waiting for transfers between devices  4.86 us (3%)
    pallas_call x1, Pallas kernels, fused_call(): pl.pallas_call(functools.partial(fused_kernel, first, parts), out_shape=[...  85.2 us
    pallas_call x1, Pallas kernels, ring_gather(): pl.pallas_call(functools.partial(ring_kernel, steps, parts, rows), out_sh...  83 us
    unnamed x2, local copies, waits for them, and re-layouts  5.38 us
    all_gather x1, waiting for transfers between devices, body(): sigma_rows = lax.all_gather(sigma_anc, 'col', axis=1, tiled=True)  4.18 us
  transfers between devices with their start and end apart: 1, of which 1 were waited for; matrix products, arithmetic and copies ran while one was open for 0% of the time, Pallas kernels for 43%

profile of v17, /device:TPU:1, one launch (start us, length us, event | category | flops | bytes accessed | tf_op | source)
XLA Modules:
  0.0 192.5 jit_solution(13049037928857148025)
XLA Ops:
  7.2 0.0 all-gather.2.cloned.1.call-start
  7.2 0.7 all-gather.2.cloned.1.call-update
  7.9 83.0 %shard_map.59 = (f32[16,16,128,128]{3,2,1,0:T(8,128)}, s32[16,3]{1,0:T(8,128)}, s32[16,3]{1,0:T(8,128)}) custom-call(s32[16,16]{1,0:T(8,128)} %struct_ref.3, f32[16,128,128]{2,1,0:T(8,128)} %bitcast.1, f32[16,128,128]{2,1,0:T(8,128)} %inv_ref.3), custom_call_target="tpu_custom_call" | custom-call | tf_op jit(solution)/shard_map/pallas_call | solution.py:91
  90.9 4.2 %all-gather.2.cloned.1.call-done.sig_ref = f32[3,48,128,128]{3,2,1,0:T(8,128)} async-done(((f32[3,3,128,128]{3,2,1,0:T(8,128)}), f32[3,48,128,128]{3,2,1,0:T(8,128)}) %all-gather.2.cloned.1.call-update) | async-done | bytes 9437200 | tf_op jit(solution)/shard_map/all_gather | solution.py:324
  95.0 85.2 %shard_map.60 = (f32[16,3,128,128]{3,2,1,0:T(8,128)}, f32[1,128,128]{2,1,0:T(8,128)}) custom-call(s32[16,16]{1,0:T(8,128)} %struct_ref.3, s32[16,3]{1,0:T(8,128)} %get-tuple-element.5.hit_ref, s32[16,3]{1,0:T(8,128)} %get-tuple-element.6.slot_ref, f32[3,48,128,128]{3,2,1,0:T(8,128)} %all-gather.2.cloned.1.call-done.sig_ref, f32[16,128,128]{2,1,0:T(8,128)} %inv_ref.3, ...), custom_call_target="tpu_custom_call" | custom-call | flops 9663676416 | bytes 26214400 | tf_op jit(solution)/shard_map/pallas_call | solution.py:284
  180.3 3.9 %copy.8 = f32[16,3,128,128]{3,2,1,0:T(8,128)} copy(f32[16,3,128,128]{3,2,1,0:T(8,128)} %get-tuple-element.10) | data formatting | bytes 6291456
  184.2 1.5 copy.9
Async XLA Ops:
  7.2 87.9 %all-gather.2.cloned.1.call-start = ((), (), s32[]{:S(2)}) async-start(), calls=%async_computation | async-start | bytes 10027008 | tf_op jit(solution)/shard_map/all_gather | solution.py:324
Sparse Core Ops, SparseCore 0:
  10.4 84.5 all-gather.1

commit v18 on v17

--- a/solution.py
+++ b/solution.py
@@ -244,8 +244,8 @@
         for j in range(rows):
             hits = hit_ref[k, j]
             slot = jnp.minimum(slot_ref[k, j], n - 1)
-            term = jnp.dot(jnp.transpose(u_vmem[slot, k]), y[j], precision=high,
-                           preferred_element_type=jnp.float32)
+            term = lax.dot_general(u_vmem[slot, k], y[j], (((0,), (0,)), ((), ())), precision=high,
+                                   preferred_element_type=jnp.float32)
             total = total + jnp.where(hits > 0, term, 0.0)
             zoff_ref[k, j] = jnp.where(hits > 0, -y[j], 0.0)
         part_ref[k] = total

time: 193 us -> 193 us (level)
  no operation moved by 1% of the time
where the time goes in v18:
time: 193 us
  Pallas kernels  168 us (87%)
  between operations  14 us (7%)
  local copies, waits for them, and re-layouts  5.38 us (3%)
  waiting for transfers between devices  4.86 us (3%)
    pallas_call x1, Pallas kernels, fused_call(): pl.pallas_call(functools.partial(fused_kernel, first, parts), out_shape=[...  85.2 us
    pallas_call x1, Pallas kernels, ring_gather(): pl.pallas_call(functools.partial(ring_kernel, steps, parts, rows), out_sh...  83 us
    unnamed x2, local copies, waits for them, and re-layouts  5.38 us
    all_gather x1, waiting for transfers between devices, body(): sigma_rows = lax.all_gather(sigma_anc, 'col', axis=1, tiled=True)  4.18 us
  transfers between devices with their start and end apart: 1, of which 1 were waited for; matrix products, arithmetic and copies ran while one was open for 0% of the time, Pallas kernels for 43%

profile of v18, /device:TPU:1, one launch (start us, length us, event | category | flops | bytes accessed | tf_op | source)
XLA Modules:
  0.0 192.5 jit_solution(13049037928857148025)
XLA Ops:
  7.2 0.0 all-gather.2.cloned.1.call-start
  7.2 0.7 all-gather.2.cloned.1.call-update
  7.9 83.0 %shard_map.59 = (f32[16,16,128,128]{3,2,1,0:T(8,128)}, s32[16,3]{1,0:T(8,128)}, s32[16,3]{1,0:T(8,128)}) custom-call(s32[16,16]{1,0:T(8,128)} %struct_ref.3, f32[16,128,128]{2,1,0:T(8,128)} %bitcast.1, f32[16,128,128]{2,1,0:T(8,128)} %inv_ref.3), custom_call_target="tpu_custom_call" | custom-call | tf_op jit(solution)/shard_map/pallas_call | solution.py:91
  90.9 4.2 %all-gather.2.cloned.1.call-done.sig_ref = f32[3,48,128,128]{3,2,1,0:T(8,128)} async-done(((f32[3,3,128,128]{3,2,1,0:T(8,128)}), f32[3,48,128,128]{3,2,1,0:T(8,128)}) %all-gather.2.cloned.1.call-update) | async-done | bytes 9437200 | tf_op jit(solution)/shard_map/all_gather | solution.py:324
  95.0 85.2 %shard_map.60 = (f32[16,3,128,128]{3,2,1,0:T(8,128)}, f32[1,128,128]{2,1,0:T(8,128)}) custom-call(s32[16,16]{1,0:T(8,128)} %struct_ref.3, s32[16,3]{1,0:T(8,128)} %get-tuple-element.5.hit_ref, s32[16,3]{1,0:T(8,128)} %get-tuple-element.6.slot_ref, f32[3,48,128,128]{3,2,1,0:T(8,128)} %all-gather.2.cloned.1.call-done.sig_ref, f32[16,128,128]{2,1,0:T(8,128)} %inv_ref.3, ...), custom_call_target="tpu_custom_call" | custom-call | flops 9663676416 | bytes 26214400 | tf_op jit(solution)/shard_map/pallas_call | solution.py:284
  180.3 3.9 %copy.8 = f32[16,3,128,128]{3,2,1,0:T(8,128)} copy(f32[16,3,128,128]{3,2,1,0:T(8,128)} %get-tuple-element.10) | data formatting | bytes 6291456
  184.2 1.5 copy.9
Async XLA Ops:
  7.2 87.9 %all-gather.2.cloned.1.call-start = ((), (), s32[]{:S(2)}) async-start(), calls=%async_computation | async-start | bytes 10027008 | tf_op jit(solution)/shard_map/all_gather | solution.py:324
Sparse Core Ops, SparseCore 0:
  10.4 84.5 all-gather.1

commit v19 on v17

--- a/solution.py
+++ b/solution.py
@@ -205,7 +205,7 @@
         load(wrap(-offset)).wait()
         load(wrap(offset)).wait()
         add_pair(wrap(-offset), wrap(offset))
-        if offset % 2 == 0 and processed < half:
+        if offset % 2 == 1 and processed < half:
             processed += 1
             ring_event(processed)
     done = first + 1

time: 193 us -> 194 us (level)
  no operation moved by 1% of the time
where the time goes in v19:
time: 194 us
  Pallas kernels  169 us (87%)
  between operations  14 us (7%)
  local copies, waits for them, and re-layouts  5.38 us (3%)
  waiting for transfers between devices  4.86 us (3%)
    pallas_call x1, Pallas kernels, fused_call(): pl.pallas_call(functools.partial(fused_kernel, first, parts), out_shape=[...  86.5 us
    pallas_call x1, Pallas kernels, ring_gather(): pl.pallas_call(functools.partial(ring_kernel, steps, parts, rows), out_sh...  83 us
    unnamed x2, local copies, waits for them, and re-layouts  5.38 us
    all_gather x1, waiting for transfers between devices, body(): sigma_rows = lax.all_gather(sigma_anc, 'col', axis=1, tiled=True)  4.18 us
  transfers between devices with their start and end apart: 1, of which 1 were waited for; matrix products, arithmetic and copies ran while one was open for 0% of the time, Pallas kernels for 43%

profile of v19, /device:TPU:1, one launch (start us, length us, event | category | flops | bytes accessed | tf_op | source)
XLA Modules:
  0.0 193.7 jit_solution(1318800219765959699)
XLA Ops:
  7.2 0.0 all-gather.2.cloned.1.call-start
  7.2 0.7 all-gather.2.cloned.1.call-update
  7.9 83.0 %shard_map.59 = (f32[16,16,128,128]{3,2,1,0:T(8,128)}, s32[16,3]{1,0:T(8,128)}, s32[16,3]{1,0:T(8,128)}) custom-call(s32[16,16]{1,0:T(8,128)} %struct_ref.3, f32[16,128,128]{2,1,0:T(8,128)} %bitcast.1, f32[16,128,128]{2,1,0:T(8,128)} %inv_ref.3), custom_call_target="tpu_custom_call" | custom-call | tf_op jit(solution)/shard_map/pallas_call | solution.py:91
  90.9 4.2 %all-gather.2.cloned.1.call-done.sig_ref = f32[3,48,128,128]{3,2,1,0:T(8,128)} async-done(((f32[3,3,128,128]{3,2,1,0:T(8,128)}), f32[3,48,128,128]{3,2,1,0:T(8,128)}) %all-gather.2.cloned.1.call-update) | async-done | bytes 9437200 | tf_op jit(solution)/shard_map/all_gather | solution.py:324
  95.0 86.5 %shard_map.60 = (f32[16,3,128,128]{3,2,1,0:T(8,128)}, f32[1,128,128]{2,1,0:T(8,128)}) custom-call(s32[16,16]{1,0:T(8,128)} %struct_ref.3, s32[16,3]{1,0:T(8,128)} %get-tuple-element.5.hit_ref, s32[16,3]{1,0:T(8,128)} %get-tuple-element.6.slot_ref, f32[3,48,128,128]{3,2,1,0:T(8,128)} %all-gather.2.cloned.1.call-done.sig_ref, f32[16,128,128]{2,1,0:T(8,128)} %inv_ref.3, ...), custom_call_target="tpu_custom_call" | custom-call | flops 9663676416 | bytes 26214400 | tf_op jit(solution)/shard_map/pallas_call | solution.py:284
  181.5 3.9 %copy.8 = f32[16,3,128,128]{3,2,1,0:T(8,128)} copy(f32[16,3,128,128]{3,2,1,0:T(8,128)} %get-tuple-element.10) | data formatting | bytes 6291456
  185.4 1.5 copy.9
Async XLA Ops:
  7.2 87.9 %all-gather.2.cloned.1.call-start = ((), (), s32[]{:S(2)}) async-start(), calls=%async_computation | async-start | bytes 10027008 | tf_op jit(solution)/shard_map/all_gather | solution.py:324
Sparse Core Ops, SparseCore 0:
  10.4 84.5 all-gather.1

commit v20 on v17

--- a/solution.py
+++ b/solution.py
@@ -322,7 +322,7 @@
 def body(sigma_anc, factor, diag_inv, struct):
     row_count = sigma_anc.shape[0]
     sigma_rows = lax.all_gather(sigma_anc, "col", axis=1, tiled=True)
-    first, parts = 6, 4
+    first, parts = 6, 2
     u_head, hit, slot = ring_gather(struct, factor[0], diag_inv, lax.axis_size("row"), row_count, first, parts)
     z_off, z_diag = fused_call(struct, hit, slot, sigma_rows, diag_inv, u_head, first, parts)
     return (z_off, z_diag)

time: 193 us -> 193 us (level)
  no operation moved by 1% of the time
where the time goes in v20:
time: 193 us; the launch traced here: 192 us
  Pallas kernels  168 us (87%)
  between operations  14 us (7%)
  local copies, waits for them, and re-layouts  5.38 us (3%)
  waiting for transfers between devices  5.32 us (3%)
    pallas_call x1, Pallas kernels, fused_call(): pl.pallas_call(functools.partial(fused_kernel, first, parts), out_shape=[...  85.1 us
    pallas_call x1, Pallas kernels, ring_gather(): pl.pallas_call(functools.partial(ring_kernel, steps, parts, rows), out_sh...  82.5 us
    unnamed x2, local copies, waits for them, and re-layouts  5.38 us
    all_gather x1, waiting for transfers between devices, body(): sigma_rows = lax.all_gather(sigma_anc, 'col', axis=1, tiled=True)  4.64 us
  transfers between devices with their start and end apart: 1, of which 1 were waited for; matrix products, arithmetic and copies ran while one was open for 0% of the time, Pallas kernels for 43%

profile of v20, /device:TPU:1, one launch (start us, length us, event | category | flops | bytes accessed | tf_op | source)
XLA Modules:
  0.0 192.3 jit_solution(3752616578752167639)
XLA Ops:
  7.2 0.0 all-gather.2.cloned.1.call-start
  7.2 0.7 all-gather.2.cloned.1.call-update
  7.9 82.5 %shard_map.59 = (f32[16,16,128,128]{3,2,1,0:T(8,128)}, s32[16,3]{1,0:T(8,128)}, s32[16,3]{1,0:T(8,128)}) custom-call(s32[16,16]{1,0:T(8,128)} %struct_ref.3, f32[16,128,128]{2,1,0:T(8,128)} %bitcast.1, f32[16,128,128]{2,1,0:T(8,128)} %inv_ref.3), custom_call_target="tpu_custom_call" | custom-call | tf_op jit(solution)/shard_map/pallas_call | solution.py:91
  90.4 4.6 %all-gather.2.cloned.1.call-done.sig_ref = f32[3,48,128,128]{3,2,1,0:T(8,128)} async-done(((f32[3,3,128,128]{3,2,1,0:T(8,128)}), f32[3,48,128,128]{3,2,1,0:T(8,128)}) %all-gather.2.cloned.1.call-update) | async-done | bytes 9437200 | tf_op jit(solution)/shard_map/all_gather | solution.py:324
  95.0 85.1 %shard_map.60 = (f32[16,3,128,128]{3,2,1,0:T(8,128)}, f32[1,128,128]{2,1,0:T(8,128)}) custom-call(s32[16,16]{1,0:T(8,128)} %struct_ref.3, s32[16,3]{1,0:T(8,128)} %get-tuple-element.5.hit_ref, s32[16,3]{1,0:T(8,128)} %get-tuple-element.6.slot_ref, f32[3,48,128,128]{3,2,1,0:T(8,128)} %all-gather.2.cloned.1.call-done.sig_ref, f32[16,128,128]{2,1,0:T(8,128)} %inv_ref.3, ...), custom_call_target="tpu_custom_call" | custom-call | flops 9663676416 | bytes 26214400 | tf_op jit(solution)/shard_map/pallas_call | solution.py:284
  180.1 3.9 %copy.8 = f32[16,3,128,128]{3,2,1,0:T(8,128)} copy(f32[16,3,128,128]{3,2,1,0:T(8,128)} %get-tuple-element.10) | data formatting | bytes 6291456
  184.0 1.5 copy.9
Async XLA Ops:
  7.2 87.9 %all-gather.2.cloned.1.call-start = ((), (), s32[]{:S(2)}) async-start(), calls=%async_computation | async-start | bytes 10027008 | tf_op jit(solution)/shard_map/all_gather | solution.py:324
Sparse Core Ops, SparseCore 0:
  10.4 84.5 all-gather.1
